TPU v7x, 32 devices: a whole 2x2x4 slice. The times are simulated.
32 devices in a mesh: seq: 4 (over y, x), outer: 8 (over z, core).
Axes of the slice: x: 2, y: 2, z: 4, core: 2. Of those that a mesh axis runs over, the one named last changes fastest.
Arguments:
- queries: bfloat16 [16384, 2048], P(('outer', 'seq')), may hold values from -41 to 41
- keys: bfloat16 [16384, 512], P(('outer', 'seq')), may hold values from -6 to 6
- values: bfloat16 [16384, 512], P(('outer', 'seq')), may hold values from -6 to 6
Outputs:
- attended: bfloat16 [16384, 2048], P(('outer', 'seq'))
All inputs are finite; a program needn't handle non-finite values.
Results may differ from a plain program's by a relative error of at most 0.014.
Values may be sent and summed in bfloat16 or wider, within the bound.
A program may use at most 64 MiB of HBM per device.

v0:
```python
import jax
import jax.numpy as jnp
from jax import lax
from jax.sharding import PartitionSpec as P

HD = 128
QHEADS = 16
KVHEADS = 4
BLOCK = 128
POOL = 8


def shortened(value):

    def short(part):
        return part.astype(jnp.bfloat16) if part.dtype == jnp.float32 else part

    return jax.tree.map(short, value)


def shifted(block, axis, distance):
    devices = range(lax.axis_size(axis))
    route = [((i - distance) % len(devices), i) for i in devices]
    return lax.ppermute(block, axis, route)


def shifted_2(value, axis, steps):
    count = lax.axis_size(axis)
    first, last = (max(0, -steps), min(count, count - steps))
    return lax.ppermute(value, axis, [(source, source + steps) for source in range(first, last)])


def pool_level(element_item):
    span_length = element_item.shape[0]
    summed = (
        element_item.astype(jnp.float32)
        .reshape(span_length // POOL, POOL, element_item.shape[1])
        .sum(axis=1)
    )
    return (summed * POOL ** (-0.5)).astype(jnp.bfloat16)


def attend_block(query_rows, key_set, value_set, valid):
    group_size = QHEADS // KVHEADS
    head_queries = query_rows.reshape(BLOCK, KVHEADS, group_size, HD).transpose(1, 0, 2, 3)
    head_keys = key_set.reshape(-1, KVHEADS, HD).transpose(1, 0, 2)
    head_values = value_set.reshape(-1, KVHEADS, HD).transpose(1, 0, 2)

    def one_head(operands):
        part_q, part_k, part_v = operands
        scores = jnp.einsum(
            "tgd,sd->gts", part_q, part_k, preferred_element_type=jnp.float32
        ) * HD ** (-0.5)
        scores = jnp.where(valid, scores, -jnp.inf)
        highest = jnp.max(scores, axis=2, keepdims=True)
        weights = jnp.exp(scores - highest)
        totals = jnp.sum(weights, axis=2)
        rounded = weights.astype(jnp.bfloat16)
        mixed = jnp.einsum("gts,sd->tgd", rounded, part_v, preferred_element_type=jnp.float32)
        return (mixed / totals.T[:, :, None]).astype(jnp.bfloat16)

    outputs = lax.map(one_head, (head_queries, head_keys, head_values))
    return outputs.transpose(1, 0, 2, 3).reshape(BLOCK, QHEADS * HD)


def auxiliary_arrays(element_items, border_width, holder_array):
    span_length = element_items[0].shape[0]
    reach_out = -(-border_width // span_length)
    bottom_pieces = []
    top_pieces = []
    for start_displacement in range(reach_out, 0, -1):
        selected_items = min(span_length, border_width - (start_displacement - 1) * span_length)
        bottom_pieces.append(
            holder_array(
                tuple(
                    (element_item[span_length - selected_items :] for element_item in element_items)
                ),
                start_displacement,
            )
        )
    for start_displacement in range(1, reach_out + 1):
        selected_items = min(span_length, border_width - (start_displacement - 1) * span_length)
        top_pieces.append(
            holder_array(
                tuple((element_item[:selected_items] for element_item in element_items)),
                -start_displacement,
            )
        )
    joined = []
    for column in range(len(element_items)):
        pieces = (
            [part[column] for part in bottom_pieces]
            + [element_items[column]]
            + [part[column] for part in top_pieces]
        )
        joined.append(jnp.concatenate(pieces, axis=0))
    return tuple(joined)


def staying_mask(start_displacement):
    seq_count = lax.axis_size("seq")
    seq_index = lax.axis_index("seq")
    if start_displacement > 0:
        return seq_index >= start_displacement
    return seq_index - start_displacement < seq_count


def token_move(element_items, start_displacement):
    within = jax.tree.map(
        lambda part, own: part.astype(own.dtype),
        shifted(shortened(element_items), "seq", start_displacement),
        element_items,
    )
    across = jax.tree.map(
        lambda part, own: part.astype(own.dtype),
        shifted_2(shortened(within), "outer", 1 if start_displacement > 0 else -1),
        within,
    )
    staying = staying_mask(start_displacement)
    return tuple((jnp.where(staying, first, second) for first, second in zip(within, across)))


def edge_move(element_items, start_displacement):
    return jax.tree.map(
        lambda part, own: part.astype(own.dtype),
        shifted_2(shortened(element_items), "outer", start_displacement),
        element_items,
    )


def group_move(element_items, start_displacement):
    return jax.tree.map(
        lambda part, own: part.astype(own.dtype),
        shifted_2(shortened(element_items), "outer", start_displacement),
        element_items,
    )


def local(queries, keys, values):
    tok_rows = queries.shape[0]
    seq_count = lax.axis_size("seq")
    outer_count = lax.axis_size("outer")
    outer_index = lax.axis_index("outer")
    linear = outer_index * seq_count + lax.axis_index("seq")
    total = tok_rows * seq_count * outer_count
    fine_k, fine_v = auxiliary_arrays((keys, values), BLOCK, token_move)
    fine_start = linear * tok_rows - BLOCK
    pooled_k = pool_level(keys)
    pooled_v = pool_level(values)
    group_k, group_v = (
        lax.all_gather(pooled_k, "seq", axis=0, tiled=True),
        lax.all_gather(pooled_v, "seq", axis=0, tiled=True),
    )
    group_len = group_k.shape[0]
    first_margin = 2 * BLOCK - min(group_len, BLOCK)
    first_k, first_v = auxiliary_arrays((group_k, group_v), first_margin, edge_move)
    first_start = outer_index * group_len - first_margin
    second_k = pool_level(group_k)
    second_v = pool_level(group_v)
    second_len = second_k.shape[0]
    second_margin = 2 * BLOCK - min(second_len, BLOCK)
    middle_k, middle_v = auxiliary_arrays((second_k, second_v), second_margin, group_move)
    middle_start = outer_index * second_len - second_margin
    top_k, top_v = (
        lax.all_gather(pool_level(second_k), "outer", axis=0, tiled=True),
        lax.all_gather(pool_level(second_v), "outer", axis=0, tiled=True),
    )
    top_mask = jnp.ones((top_k.shape[0],), dtype=bool)
    buffers = [
        (fine_k, fine_v, fine_start, total),
        (first_k, first_v, first_start, total // POOL),
        (middle_k, middle_v, middle_start, total // POOL**2),
    ]
    local_blocks = tok_rows // BLOCK

    def one_block(local_block):
        fine_index = linear * local_blocks + local_block
        key_parts = []
        value_parts = []
        mask_parts = []
        for level_index in range(3):
            level_k, level_v, level_start, level_len = buffers[level_index]
            coarse = fine_index // POOL**level_index
            start_row = (coarse - 1) * BLOCK - level_start
            key_parts.append(lax.dynamic_slice_in_dim(level_k, start_row, 3 * BLOCK, 0))
            value_parts.append(lax.dynamic_slice_in_dim(level_v, start_row, 3 * BLOCK, 0))
            positions = (coarse - 1) * BLOCK + jnp.arange(3 * BLOCK, dtype=jnp.int32)
            mask_parts.append((positions >= 0) & (positions < level_len))
        key_parts.append(top_k)
        value_parts.append(top_v)
        mask_parts.append(top_mask)
        query_rows = lax.dynamic_slice_in_dim(queries, local_block * BLOCK, BLOCK, 0)
        return attend_block(
            query_rows,
            jnp.concatenate(key_parts, axis=0),
            jnp.concatenate(value_parts, axis=0),
            jnp.concatenate(mask_parts, axis=0),
        )

    result = lax.map(one_block, jnp.arange(local_blocks, dtype=jnp.int32))
    return result.reshape(tok_rows, QHEADS * HD)


def solution(mesh):
    placed = (P(("outer", "seq"), None), P(("outer", "seq"), None), P(("outer", "seq"), None))
    return jax.shard_map(
        local, mesh=mesh, in_specs=placed, out_specs=P(("outer", "seq"), None), check_vma=False
    )
```

profile of v0, /device:TPU:26, one launch (start us, length us, event | category | flops | bytes accessed | tf_op | source)
XLA Modules:
  0.0 262.8 jit_solution(16759093504780457326)
XLA Ops:
  0.0 1.5 convert_reduce_fusion
  1.5 9.0 %all_gather.14 = bf16[256,512]{1,0:T(8,128)(2,1)S(1)} all-gather(bf16[64,512]{1,0:T(8,128)(2,1)S(1)} %multiply_convert_fusion), channel_id=1, replica_groups=mesh['seq'=4,'outer'=8] {'seq'}, dimensions={0}, use_global_device_ids=true | all-gather | bytes 327680 | tf_op jit(solution)/shard_map/all_gather | solution.py:152
  11.4 1.3 collective-permute-start.27
  12.7 1.3 collective-permute-start.28
  14.0 1.3 collective-permute-start.29
  16.6 1.4 convert_reduce_fusion.1
  18.1 8.1 %all_gather.12 = bf16[256,512]{1,0:T(8,128)(2,1)S(1)} all-gather(bf16[64,512]{1,0:T(8,128)(2,1)S(1)} %multiply_convert_fusion.1), channel_id=1, replica_groups=mesh['seq'=4,'outer'=8] {'seq'}, dimensions={0}, use_global_device_ids=true | all-gather | bytes 327680 | tf_op jit(solution)/shard_map/all_gather | solution.py:151
  26.5 15.1 %all-gather = bf16[8,4,512]{2,1,0:T(4,128)(2,1)S(1)} all-gather(bf16[1,4,512]{2,1,0:T(4,128)(2,1)S(1)} %fusion.39), channel_id=1, replica_groups=mesh['seq'=4,'outer'=8] {'outer'}, dimensions={0}, use_global_device_ids=true | all-gather | bytes 36864 | tf_op jit(solution)/shard_map/all_gather | solution.py:165
  41.7 14.1 %all-gather.1 = bf16[8,4,512]{2,1,0:T(4,128)(2,1)S(1)} all-gather(bf16[1,4,512]{2,1,0:T(4,128)(2,1)S(1)} %fusion.40), channel_id=1, replica_groups=mesh['seq'=4,'outer'=8] {'outer'}, dimensions={0}, use_global_device_ids=true | all-gather | bytes 36864 | tf_op jit(solution)/shard_map/all_gather | solution.py:166
  57.7 2.2 collective-permute-start.32
  60.5 3.9 %collective-permute-start.33 = (bf16[32,512]{1,0:T(8,128)(2,1)S(1)}, bf16[32,512]{1,0:T(8,128)(2,1)S(1)}, u32[]{:S(2)}, u32[]{:S(2)}) collective-permute-start(bf16[32,512]{1,0:T(8,128)(2,1)S(1)} %get-tuple-element.380), channel_id=1, source_target_pairs={{1,0},{2,1},{3,2},{4,3},{5,4},{6,5},{7,6},{9,8},{10,9},{11,10},{12... | collective-permute-start | bytes 98312 | tf_op jit(solution)/shard_map/ppermute | solution.py:30
  65.0 4.0 %collective-permute-start.34 = (bf16[32,512]{1,0:T(8,128)(2,1)S(1)}, bf16[32,512]{1,0:T(8,128)(2,1)S(1)}, u32[]{:S(2)}, u32[]{:S(2)}) collective-permute-start(bf16[32,512]{1,0:T(8,128)(2,1)S(1)} %get-tuple-element.380), channel_id=1, source_target_pairs={{2,0},{3,1},{4,2},{5,3},{6,4},{7,5},{10,8},{11,9},{12,10},{13,11},... | collective-permute-start | bytes 98312 | tf_op jit(solution)/shard_map/ppermute | solution.py:30
  69.6 2.6 collective-permute-start.35
  72.8 1.6 collective-permute-start.36
  78.8 7.0 %collective-permute-done.7 = bf16[32,512]{1,0:T(8,128)(2,1)S(1)} collective-permute-done((bf16[32,512]{1,0:T(8,128)(2,1)S(1)}, bf16[32,512]{1,0:T(8,128)(2,1)S(1)}, u32[]{:S(2)}, u32[]{:S(2)}) %collective-permute-start.7) | collective-permute-done | bytes 32800 | tf_op jit(solution)/shard_map/ppermute | solution.py:30
  87.6 5.1 %collective-permute-done.8 = bf16[32,512]{1,0:T(8,128)(2,1)S(1)} collective-permute-done((bf16[32,512]{1,0:T(8,128)(2,1)S(1)}, bf16[32,512]{1,0:T(8,128)(2,1)S(1)}, u32[]{:S(2)}, u32[]{:S(2)}) %collective-permute-start.8) | collective-permute-done | bytes 32800 | tf_op jit(solution)/shard_map/ppermute | solution.py:30
  94.6 4.8 %collective-permute-done.9 = bf16[32,512]{1,0:T(8,128)(2,1)S(1)} collective-permute-done((bf16[32,512]{1,0:T(8,128)(2,1)S(1)}, bf16[32,512]{1,0:T(8,128)(2,1)S(1)}, u32[]{:S(2)}, u32[]{:S(2)}) %collective-permute-start.9) | collective-permute-done | bytes 32800 | tf_op jit(solution)/shard_map/ppermute | solution.py:30
  101.3 4.2 %collective-permute-done.10 = bf16[32,512]{1,0:T(8,128)(2,1)S(1)} collective-permute-done((bf16[32,512]{1,0:T(8,128)(2,1)S(1)}, bf16[32,512]{1,0:T(8,128)(2,1)S(1)}, u32[]{:S(2)}, u32[]{:S(2)}) %collective-permute-start.10) | collective-permute-done | bytes 32800 | tf_op jit(solution)/shard_map/ppermute | solution.py:30
  107.4 3.9 %collective-permute-done.11 = bf16[32,512]{1,0:T(8,128)(2,1)S(1)} collective-permute-done((bf16[32,512]{1,0:T(8,128)(2,1)S(1)}, bf16[32,512]{1,0:T(8,128)(2,1)S(1)}, u32[]{:S(2)}, u32[]{:S(2)}) %collective-permute-start.11) | collective-permute-done | bytes 32800 | tf_op jit(solution)/shard_map/ppermute | solution.py:30
  111.3 1.9 collective-permute-start.12
  113.9 2.7 %collective-permute-done.12 = bf16[32,512]{1,0:T(8,128)(2,1)S(1)} collective-permute-done((bf16[32,512]{1,0:T(8,128)(2,1)S(1)}, bf16[32,512]{1,0:T(8,128)(2,1)S(1)}, u32[]{:S(2)}, u32[]{:S(2)}) %collective-permute-start.12) | collective-permute-done | bytes 32800 | tf_op jit(solution)/shard_map/ppermute | solution.py:30
  122.2 1.9 collective-permute-start.13
  126.7 1.5 collective-permute-start.15
  135.7 1.5 collective-permute-start.2
  137.8 1.4 collective-permute-start
  139.9 2.7 %collective-permute-start.4 = (bf16[128,512]{1,0:T(8,128)(2,1)S(1)}, bf16[128,512]{1,0:T(8,128)(2,1)S(1)}, u32[]{:S(2)}, u32[]{:S(2)}) collective-permute-start(bf16[128,512]{1,0:T(8,128)(2,1)S(1)} %get-tuple-element.395), channel_id=1, source_target_pairs={{0,1},{1,2},{2,3},{3,4},{4,5},{5,6},{6,7},{8,9},{9,10},{10,11},{11... | collective-permute-start | bytes 393224 | tf_op jit(solution)/shard_map/ppermute | solution.py:30
  143.2 2.8 %collective-permute-start.5 = (bf16[128,512]{1,0:T(8,128)(2,1)S(1)}, bf16[128,512]{1,0:T(8,128)(2,1)S(1)}, u32[]{:S(2)}, u32[]{:S(2)}) collective-permute-start(bf16[128,512]{1,0:T(8,128)(2,1)S(1)} %get-tuple-element.396), channel_id=1, source_target_pairs={{1,0},{2,1},{3,2},{4,3},{5,4},{6,5},{7,6},{9,8},{10,9},{11,10},{12... | collective-permute-start | bytes 393224 | tf_op jit(solution)/shard_map/ppermute | solution.py:30
  147.2 2.3 collective-permute-start.20
  149.6 1.9 collective-permute-start.24
  151.5 3.6 %collective-permute-start.25 = (bf16[128,512]{1,0:T(8,128)(2,1)S(1)}, bf16[128,512]{1,0:T(8,128)(2,1)S(1)}, u32[]{:S(2)}, u32[]{:S(2)}) collective-permute-start(bf16[128,512]{1,0:T(8,128)(2,1)S(1)} %get-tuple-element.394), channel_id=1, source_target_pairs={{1,0},{2,1},{3,2},{4,3},{5,4},{6,5},{7,6},{9,8},{10,9},{11,10},{12... | collective-permute-start | bytes 393224 | tf_op jit(solution)/shard_map/ppermute | solution.py:30
  155.8 1.9 collective-permute-start.3
  158.5 2.4 collective-permute-start.1
  160.9 3.2 %collective-permute-start.23 = (bf16[128,512]{1,0:T(8,128)(2,1)S(1)}, bf16[128,512]{1,0:T(8,128)(2,1)S(1)}, u32[]{:S(2)}, u32[]{:S(2)}) collective-permute-start(bf16[128,512]{1,0:T(8,128)(2,1)S(1)} %collective-permute-done.22), channel_id=1, source_target_pairs={{1,0},{2,1},{3,2},{4,3},{5,4},{6,5},{7,6},{9,8},{10,9},{11,10},{12... | collective-permute-start | bytes 393224 | tf_op jit(solution)/shard_map/ppermute | solution.py:30
  164.1 1.9 collective-permute-start.21
  167.9 2.5 collective-permute-done.21
  171.4 91.5 %while.36 = (s32[]{:T(128)}, bf16[4,128,2048]{2,1,0:T(8,128)(2,1)}, s32[4]{0:T(128)S(1)}, bf16[512,2048]{1,0:T(8,128)(2,1)}, s32[]{:T(128)}, /*index=5*/s32[]{:T...) while((s32[]{:T(128)}, bf16[4,128,2048]{2,1,0:T(8,128)(2,1)}, ...), condition=%wide.region_11.12_spmd, body=%wide.region_6.11_spmd.sunk | while | flops 324459552 | bytes 31624100 | solution.py:200
  180.5 3.4 %reshape.94 = bf16[1184,4,128]{2,1,0:T(4,128)(2,1)} reshape(bf16[1184,512]{1,0:T(8,128)(2,1)} %get-tuple-element.547) | data formatting | bytes 2424832 | tf_op jit(solution)/shard_map/while/body/eval_jaxpr/reshape | solution.py:46
  183.9 1.4 copy.24
  187.4 5.8 %while.37 = (s32[]{:T(128)}, bf16[4,128,4,128]{1,3,2,0:T(8,128)(2,1)S(1)}, bf16[4,1184,128]{2,1,0:T(8,128)(2,1)S(1)}, pred[1184]{0:T(1024)(128)(4,1)S(1)}, bf16[...) while((s32[]{:T(128)}, bf16[4,128,4,128]{1,3,2,0:T(8,128)(2,1)S(1)}, ...), condition=%wide.region_10.10_spmd, body=%wide.region_7.9_spmd.sunk | while | flops 314752000 | bytes 8157261 | solution.py:62
  203.3 3.4 %reshape.94 = bf16[1184,4,128]{2,1,0:T(4,128)(2,1)} reshape(bf16[1184,512]{1,0:T(8,128)(2,1)} %get-tuple-element.547) | data formatting | bytes 2424832 | tf_op jit(solution)/shard_map/while/body/eval_jaxpr/reshape | solution.py:46
  206.8 1.4 copy.24
  210.3 5.8 %while.37 = (s32[]{:T(128)}, bf16[4,128,4,128]{1,3,2,0:T(8,128)(2,1)S(1)}, bf16[4,1184,128]{2,1,0:T(8,128)(2,1)S(1)}, pred[1184]{0:T(1024)(128)(4,1)S(1)}, bf16[...) while((s32[]{:T(128)}, bf16[4,128,4,128]{1,3,2,0:T(8,128)(2,1)S(1)}, ...), condition=%wide.region_10.10_spmd, body=%wide.region_7.9_spmd.sunk | while | flops 314752000 | bytes 8157261 | solution.py:62
  226.2 3.4 %reshape.94 = bf16[1184,4,128]{2,1,0:T(4,128)(2,1)} reshape(bf16[1184,512]{1,0:T(8,128)(2,1)} %get-tuple-element.547) | data formatting | bytes 2424832 | tf_op jit(solution)/shard_map/while/body/eval_jaxpr/reshape | solution.py:46
  229.6 1.4 copy.24
  233.1 5.8 %while.37 = (s32[]{:T(128)}, bf16[4,128,4,128]{1,3,2,0:T(8,128)(2,1)S(1)}, bf16[4,1184,128]{2,1,0:T(8,128)(2,1)S(1)}, pred[1184]{0:T(1024)(128)(4,1)S(1)}, bf16[...) while((s32[]{:T(128)}, bf16[4,128,4,128]{1,3,2,0:T(8,128)(2,1)S(1)}, ...), condition=%wide.region_10.10_spmd, body=%wide.region_7.9_spmd.sunk | while | flops 314752000 | bytes 8157261 | solution.py:62
  249.1 3.4 %reshape.94 = bf16[1184,4,128]{2,1,0:T(4,128)(2,1)} reshape(bf16[1184,512]{1,0:T(8,128)(2,1)} %get-tuple-element.547) | data formatting | bytes 2424832 | tf_op jit(solution)/shard_map/while/body/eval_jaxpr/reshape | solution.py:46
  252.5 1.4 copy.24
  256.0 5.8 %while.37 = (s32[]{:T(128)}, bf16[4,128,4,128]{1,3,2,0:T(8,128)(2,1)S(1)}, bf16[4,1184,128]{2,1,0:T(8,128)(2,1)S(1)}, pred[1184]{0:T(1024)(128)(4,1)S(1)}, bf16[...) while((s32[]{:T(128)}, bf16[4,128,4,128]{1,3,2,0:T(8,128)(2,1)S(1)}, ...), condition=%wide.region_10.10_spmd, body=%wide.region_7.9_spmd.sunk | while | flops 314752000 | bytes 8157261 | solution.py:62
  (233 shorter events, 108.1 us)
Async XLA Ops:
  0.0 18.0 %copy-start.1 = (bf16[512,512]{1,0:T(8,128)(2,1)S(1)}, bf16[512,512]{1,0:T(8,128)(2,1)}, u32[]{:S(2)}) copy-start(bf16[512,512]{1,0:T(8,128)(2,1)} %param.9) | copy-start | bytes 1572868
  0.0 18.0 %copy-start = (bf16[512,512]{1,0:T(8,128)(2,1)S(1)}, bf16[512,512]{1,0:T(8,128)(2,1)}, u32[]{:S(2)}) copy-start(bf16[512,512]{1,0:T(8,128)(2,1)} %param.8) | copy-start | bytes 1572868
  10.7 45.1 %collective-permute-start.26 = (bf16[32,512]{1,0:T(8,128)(2,1)S(1)}, bf16[32,512]{1,0:T(8,128)(2,1)S(1)}, u32[]{:S(2)}, u32[]{:S(2)}) collective-permute-start(bf16[32,512]{1,0:T(8,128)(2,1)S(1)} %get-tuple-element.380), channel_id=1, source_target_pairs={{0,7},{8,15},{16,23},{24,31}} | collective-permute-start | bytes 98312 | tf_op jit(solution)/shard_map/ppermute | solution.py:30
  11.4 46.3 %collective-permute-start.27 = (bf16[32,512]{1,0:T(8,128)(2,1)S(1)}, bf16[32,512]{1,0:T(8,128)(2,1)S(1)}, u32[]{:S(2)}, u32[]{:S(2)}) collective-permute-start(bf16[32,512]{1,0:T(8,128)(2,1)S(1)} %get-tuple-element.380), channel_id=1, source_target_pairs={{0,6},{1,7},{8,14},{9,15},{16,22},{17,23},{24,30},{25,31}} | collective-permute-start | bytes 98312 | tf_op jit(solution)/shard_map/ppermute | solution.py:30
  12.7 47.9 %collective-permute-start.28 = (bf16[32,512]{1,0:T(8,128)(2,1)S(1)}, bf16[32,512]{1,0:T(8,128)(2,1)S(1)}, u32[]{:S(2)}, u32[]{:S(2)}) collective-permute-start(bf16[32,512]{1,0:T(8,128)(2,1)S(1)} %get-tuple-element.380), channel_id=1, source_target_pairs={{0,5},{1,6},{2,7},{8,13},{9,14},{10,15},{16,21},{17,22},{18,23},{2... | collective-permute-start | bytes 98312 | tf_op jit(solution)/shard_map/ppermute | solution.py:30
  14.0 51.1 %collective-permute-start.29 = (bf16[32,512]{1,0:T(8,128)(2,1)S(1)}, bf16[32,512]{1,0:T(8,128)(2,1)S(1)}, u32[]{:S(2)}, u32[]{:S(2)}) collective-permute-start(bf16[32,512]{1,0:T(8,128)(2,1)S(1)} %get-tuple-element.380), channel_id=1, source_target_pairs={{0,4},{1,5},{2,6},{3,7},{8,12},{9,13},{10,14},{11,15},{16,20},{17,... | collective-permute-start | bytes 98312 | tf_op jit(solution)/shard_map/ppermute | solution.py:30
  15.3 54.3 %collective-permute-start.30 = (bf16[32,512]{1,0:T(8,128)(2,1)S(1)}, bf16[32,512]{1,0:T(8,128)(2,1)S(1)}, u32[]{:S(2)}, u32[]{:S(2)}) collective-permute-start(bf16[32,512]{1,0:T(8,128)(2,1)S(1)} %get-tuple-element.380), channel_id=1, source_target_pairs={{0,3},{1,4},{2,5},{3,6},{4,7},{8,11},{9,12},{10,13},{11,14},{12,15... | collective-permute-start | bytes 98312 | tf_op jit(solution)/shard_map/ppermute | solution.py:30
  55.8 17.0 %collective-permute-start.31 = (bf16[32,512]{1,0:T(8,128)(2,1)S(1)}, bf16[32,512]{1,0:T(8,128)(2,1)S(1)}, u32[]{:S(2)}, u32[]{:S(2)}) collective-permute-start(bf16[32,512]{1,0:T(8,128)(2,1)S(1)} %get-tuple-element.380), channel_id=1, source_target_pairs={{0,2},{1,3},{2,4},{3,5},{4,6},{5,7},{8,10},{9,11},{10,12},{11,13},... | collective-permute-start | bytes 98312 | tf_op jit(solution)/shard_map/ppermute | solution.py:30
  57.7 17.3 %collective-permute-start.32 = (bf16[32,512]{1,0:T(8,128)(2,1)S(1)}, bf16[32,512]{1,0:T(8,128)(2,1)S(1)}, u32[]{:S(2)}, u32[]{:S(2)}) collective-permute-start(bf16[32,512]{1,0:T(8,128)(2,1)S(1)} %get-tuple-element.380), channel_id=1, source_target_pairs={{0,1},{1,2},{2,3},{3,4},{4,5},{5,6},{6,7},{8,9},{9,10},{10,11},{11... | collective-permute-start | bytes 98312 | tf_op jit(solution)/shard_map/ppermute | solution.py:30
  60.5 58.5 %collective-permute-start.33 = (bf16[32,512]{1,0:T(8,128)(2,1)S(1)}, bf16[32,512]{1,0:T(8,128)(2,1)S(1)}, u32[]{:S(2)}, u32[]{:S(2)}) collective-permute-start(bf16[32,512]{1,0:T(8,128)(2,1)S(1)} %get-tuple-element.380), channel_id=1, source_target_pairs={{1,0},{2,1},{3,2},{4,3},{5,4},{6,5},{7,6},{9,8},{10,9},{11,10},{12... | collective-permute-start | bytes 98312 | tf_op jit(solution)/shard_map/ppermute | solution.py:30
  65.0 55.9 %collective-permute-start.34 = (bf16[32,512]{1,0:T(8,128)(2,1)S(1)}, bf16[32,512]{1,0:T(8,128)(2,1)S(1)}, u32[]{:S(2)}, u32[]{:S(2)}) collective-permute-start(bf16[32,512]{1,0:T(8,128)(2,1)S(1)} %get-tuple-element.380), channel_id=1, source_target_pairs={{2,0},{3,1},{4,2},{5,3},{6,4},{7,5},{10,8},{11,9},{12,10},{13,11},... | collective-permute-start | bytes 98312 | tf_op jit(solution)/shard_map/ppermute | solution.py:30
  69.6 52.6 %collective-permute-start.35 = (bf16[32,512]{1,0:T(8,128)(2,1)S(1)}, bf16[32,512]{1,0:T(8,128)(2,1)S(1)}, u32[]{:S(2)}, u32[]{:S(2)}) collective-permute-start(bf16[32,512]{1,0:T(8,128)(2,1)S(1)} %get-tuple-element.380), channel_id=1, source_target_pairs={{3,0},{4,1},{5,2},{6,3},{7,4},{11,8},{12,9},{13,10},{14,11},{15,12... | collective-permute-start | bytes 98312 | tf_op jit(solution)/shard_map/ppermute | solution.py:30
  72.8 52.0 %collective-permute-start.36 = (bf16[32,512]{1,0:T(8,128)(2,1)S(1)}, bf16[32,512]{1,0:T(8,128)(2,1)S(1)}, u32[]{:S(2)}, u32[]{:S(2)}) collective-permute-start(bf16[32,512]{1,0:T(8,128)(2,1)S(1)} %get-tuple-element.380), channel_id=1, source_target_pairs={{4,0},{5,1},{6,2},{7,3},{12,8},{13,9},{14,10},{15,11},{20,16},{21,... | collective-permute-start | bytes 98312 | tf_op jit(solution)/shard_map/ppermute | solution.py:30
  75.0 1.9 collective-permute-start.6
  76.8 8.9 %collective-permute-start.7 = (bf16[32,512]{1,0:T(8,128)(2,1)S(1)}, bf16[32,512]{1,0:T(8,128)(2,1)S(1)}, u32[]{:S(2)}, u32[]{:S(2)}) collective-permute-start(bf16[32,512]{1,0:T(8,128)(2,1)S(1)} %get-tuple-element.382), channel_id=1, source_target_pairs={{0,6},{1,7},{8,14},{9,15},{16,22},{17,23},{24,30},{25,31}} | collective-permute-start | bytes 98312 | tf_op jit(solution)/shard_map/ppermute | solution.py:30
  85.7 7.0 %collective-permute-start.8 = (bf16[32,512]{1,0:T(8,128)(2,1)S(1)}, bf16[32,512]{1,0:T(8,128)(2,1)S(1)}, u32[]{:S(2)}, u32[]{:S(2)}) collective-permute-start(bf16[32,512]{1,0:T(8,128)(2,1)S(1)} %get-tuple-element.382), channel_id=1, source_target_pairs={{0,5},{1,6},{2,7},{8,13},{9,14},{10,15},{16,21},{17,22},{18,23},{2... | collective-permute-start | bytes 98312 | tf_op jit(solution)/shard_map/ppermute | solution.py:30
  92.7 6.7 %collective-permute-start.9 = (bf16[32,512]{1,0:T(8,128)(2,1)S(1)}, bf16[32,512]{1,0:T(8,128)(2,1)S(1)}, u32[]{:S(2)}, u32[]{:S(2)}) collective-permute-start(bf16[32,512]{1,0:T(8,128)(2,1)S(1)} %get-tuple-element.382), channel_id=1, source_target_pairs={{0,4},{1,5},{2,6},{3,7},{8,12},{9,13},{10,14},{11,15},{16,20},{17,... | collective-permute-start | bytes 98312 | tf_op jit(solution)/shard_map/ppermute | solution.py:30
  99.4 6.1 %collective-permute-start.10 = (bf16[32,512]{1,0:T(8,128)(2,1)S(1)}, bf16[32,512]{1,0:T(8,128)(2,1)S(1)}, u32[]{:S(2)}, u32[]{:S(2)}) collective-permute-start(bf16[32,512]{1,0:T(8,128)(2,1)S(1)} %get-tuple-element.382), channel_id=1, source_target_pairs={{0,3},{1,4},{2,5},{3,6},{4,7},{8,11},{9,12},{10,13},{11,14},{12,15... | collective-permute-start | bytes 98312 | tf_op jit(solution)/shard_map/ppermute | solution.py:30
  105.5 5.8 %collective-permute-start.11 = (bf16[32,512]{1,0:T(8,128)(2,1)S(1)}, bf16[32,512]{1,0:T(8,128)(2,1)S(1)}, u32[]{:S(2)}, u32[]{:S(2)}) collective-permute-start(bf16[32,512]{1,0:T(8,128)(2,1)S(1)} %get-tuple-element.382), channel_id=1, source_target_pairs={{0,2},{1,3},{2,4},{3,5},{4,6},{5,7},{8,10},{9,11},{10,12},{11,13},... | collective-permute-start | bytes 98312 | tf_op jit(solution)/shard_map/ppermute | solution.py:30
  111.3 5.2 %collective-permute-start.12 = (bf16[32,512]{1,0:T(8,128)(2,1)S(1)}, bf16[32,512]{1,0:T(8,128)(2,1)S(1)}, u32[]{:S(2)}, u32[]{:S(2)}) collective-permute-start(bf16[32,512]{1,0:T(8,128)(2,1)S(1)} %get-tuple-element.382), channel_id=1, source_target_pairs={{0,1},{1,2},{2,3},{3,4},{4,5},{5,6},{6,7},{8,9},{9,10},{10,11},{11... | collective-permute-start | bytes 98312 | tf_op jit(solution)/shard_map/ppermute | solution.py:30
  116.6 10.1 %collective-permute-start.37 = (bf16[32,512]{1,0:T(8,128)(2,1)S(1)}, bf16[32,512]{1,0:T(8,128)(2,1)S(1)}, u32[]{:S(2)}, u32[]{:S(2)}) collective-permute-start(bf16[32,512]{1,0:T(8,128)(2,1)S(1)} %get-tuple-element.380), channel_id=1, source_target_pairs={{5,0},{6,1},{7,2},{13,8},{14,9},{15,10},{21,16},{22,17},{23,18},{2... | collective-permute-start | bytes 98312 | tf_op jit(solution)/shard_map/ppermute | solution.py:30
  119.1 9.7 %collective-permute-start.38 = (bf16[32,512]{1,0:T(8,128)(2,1)S(1)}, bf16[32,512]{1,0:T(8,128)(2,1)S(1)}, u32[]{:S(2)}, u32[]{:S(2)}) collective-permute-start(bf16[32,512]{1,0:T(8,128)(2,1)S(1)} %get-tuple-element.380), channel_id=1, source_target_pairs={{6,0},{7,1},{14,8},{15,9},{22,16},{23,17},{30,24},{31,25}} | collective-permute-start | bytes 98312 | tf_op jit(solution)/shard_map/ppermute | solution.py:30
  121.0 9.7 %collective-permute-start.39 = (bf16[32,512]{1,0:T(8,128)(2,1)S(1)}, bf16[32,512]{1,0:T(8,128)(2,1)S(1)}, u32[]{:S(2)}, u32[]{:S(2)}) collective-permute-start(bf16[32,512]{1,0:T(8,128)(2,1)S(1)} %get-tuple-element.380), channel_id=1, source_target_pairs={{7,0},{15,8},{23,16},{31,24}} | collective-permute-start | bytes 98312 | tf_op jit(solution)/shard_map/ppermute | solution.py:30
  122.2 10.3 %collective-permute-start.13 = (bf16[32,512]{1,0:T(8,128)(2,1)S(1)}, bf16[32,512]{1,0:T(8,128)(2,1)S(1)}, u32[]{:S(2)}, u32[]{:S(2)}) collective-permute-start(bf16[32,512]{1,0:T(8,128)(2,1)S(1)} %get-tuple-element.382), channel_id=1, source_target_pairs={{1,0},{2,1},{3,2},{4,3},{5,4},{6,5},{7,6},{9,8},{10,9},{11,10},{12... | collective-permute-start | bytes 98312 | tf_op jit(solution)/shard_map/ppermute | solution.py:30
  124.8 9.7 %collective-permute-start.14 = (bf16[32,512]{1,0:T(8,128)(2,1)S(1)}, bf16[32,512]{1,0:T(8,128)(2,1)S(1)}, u32[]{:S(2)}, u32[]{:S(2)}) collective-permute-start(bf16[32,512]{1,0:T(8,128)(2,1)S(1)} %get-tuple-element.382), channel_id=1, source_target_pairs={{2,0},{3,1},{4,2},{5,3},{6,4},{7,5},{10,8},{11,9},{12,10},{13,11},... | collective-permute-start | bytes 98312 | tf_op jit(solution)/shard_map/ppermute | solution.py:30
  126.7 9.1 %collective-permute-start.15 = (bf16[32,512]{1,0:T(8,128)(2,1)S(1)}, bf16[32,512]{1,0:T(8,128)(2,1)S(1)}, u32[]{:S(2)}, u32[]{:S(2)}) collective-permute-start(bf16[32,512]{1,0:T(8,128)(2,1)S(1)} %get-tuple-element.382), channel_id=1, source_target_pairs={{3,0},{4,1},{5,2},{6,3},{7,4},{11,8},{12,9},{13,10},{14,11},{15,12... | collective-permute-start | bytes 98312 | tf_op jit(solution)/shard_map/ppermute | solution.py:30
  128.8 9.1 %collective-permute-start.16 = (bf16[32,512]{1,0:T(8,128)(2,1)S(1)}, bf16[32,512]{1,0:T(8,128)(2,1)S(1)}, u32[]{:S(2)}, u32[]{:S(2)}) collective-permute-start(bf16[32,512]{1,0:T(8,128)(2,1)S(1)} %get-tuple-element.382), channel_id=1, source_target_pairs={{4,0},{5,1},{6,2},{7,3},{12,8},{13,9},{14,10},{15,11},{20,16},{21,... | collective-permute-start | bytes 98312 | tf_op jit(solution)/shard_map/ppermute | solution.py:30
  130.7 9.2 %collective-permute-start.17 = (bf16[32,512]{1,0:T(8,128)(2,1)S(1)}, bf16[32,512]{1,0:T(8,128)(2,1)S(1)}, u32[]{:S(2)}, u32[]{:S(2)}) collective-permute-start(bf16[32,512]{1,0:T(8,128)(2,1)S(1)} %get-tuple-element.382), channel_id=1, source_target_pairs={{5,0},{6,1},{7,2},{13,8},{14,9},{15,10},{21,16},{22,17},{23,18},{2... | collective-permute-start | bytes 98312 | tf_op jit(solution)/shard_map/ppermute | solution.py:30
  132.6 10.6 %collective-permute-start.18 = (bf16[32,512]{1,0:T(8,128)(2,1)S(1)}, bf16[32,512]{1,0:T(8,128)(2,1)S(1)}, u32[]{:S(2)}, u32[]{:S(2)}) collective-permute-start(bf16[32,512]{1,0:T(8,128)(2,1)S(1)} %get-tuple-element.382), channel_id=1, source_target_pairs={{6,0},{7,1},{14,8},{15,9},{22,16},{23,17},{30,24},{31,25}} | collective-permute-start | bytes 98312 | tf_op jit(solution)/shard_map/ppermute | solution.py:30
  134.5 12.2 %collective-permute-start.19 = (bf16[32,512]{1,0:T(8,128)(2,1)S(1)}, bf16[32,512]{1,0:T(8,128)(2,1)S(1)}, u32[]{:S(2)}, u32[]{:S(2)}) collective-permute-start(bf16[32,512]{1,0:T(8,128)(2,1)S(1)} %get-tuple-element.382), channel_id=1, source_target_pairs={{7,0},{15,8},{23,16},{31,24}} | collective-permute-start | bytes 98312 | tf_op jit(solution)/shard_map/ppermute | solution.py:30
  135.7 11.5 %collective-permute-start.2 = (bf16[128,512]{1,0:T(8,128)(2,1)S(1)}, bf16[128,512]{1,0:T(8,128)(2,1)S(1)}, u32[]{:S(2)}, u32[]{:S(2)}) collective-permute-start(bf16[128,512]{1,0:T(8,128)(2,1)S(1)} %get-tuple-element.392), channel_id=1, source_target_pairs={{8,0},{16,8},{24,16},{0,24},{9,1},{17,9},{25,17},{1,25},{10,2},{18... | collective-permute-start | bytes 393224 | tf_op jit(solution)/shard_map/ppermute | solution.py:24
  137.8 11.7 %collective-permute-start = (bf16[128,512]{1,0:T(8,128)(2,1)S(1)}, bf16[128,512]{1,0:T(8,128)(2,1)S(1)}, u32[]{:S(2)}, u32[]{:S(2)}) collective-permute-start(bf16[128,512]{1,0:T(8,128)(2,1)S(1)} %get-tuple-element.391), channel_id=1, source_target_pairs={{24,0},{0,8},{8,16},{16,24},{25,1},{1,9},{9,17},{17,25},{26,2},{2,... | collective-permute-start | bytes 393224 | tf_op jit(solution)/shard_map/ppermute | solution.py:24
  139.9 11.6 %collective-permute-start.4 = (bf16[128,512]{1,0:T(8,128)(2,1)S(1)}, bf16[128,512]{1,0:T(8,128)(2,1)S(1)}, u32[]{:S(2)}, u32[]{:S(2)}) collective-permute-start(bf16[128,512]{1,0:T(8,128)(2,1)S(1)} %get-tuple-element.395), channel_id=1, source_target_pairs={{0,1},{1,2},{2,3},{3,4},{4,5},{5,6},{6,7},{8,9},{9,10},{10,11},{11... | collective-permute-start | bytes 393224 | tf_op jit(solution)/shard_map/ppermute | solution.py:30
  143.2 12.6 %collective-permute-start.5 = (bf16[128,512]{1,0:T(8,128)(2,1)S(1)}, bf16[128,512]{1,0:T(8,128)(2,1)S(1)}, u32[]{:S(2)}, u32[]{:S(2)}) collective-permute-start(bf16[128,512]{1,0:T(8,128)(2,1)S(1)} %get-tuple-element.396), channel_id=1, source_target_pairs={{1,0},{2,1},{3,2},{4,3},{5,4},{6,5},{7,6},{9,8},{10,9},{11,10},{12... | collective-permute-start | bytes 393224 | tf_op jit(solution)/shard_map/ppermute | solution.py:30
  146.6 11.9 %collective-permute-start.22 = (bf16[128,512]{1,0:T(8,128)(2,1)S(1)}, bf16[128,512]{1,0:T(8,128)(2,1)S(1)}, u32[]{:S(2)}, u32[]{:S(2)}) collective-permute-start(bf16[128,512]{1,0:T(8,128)(2,1)S(1)} %get-tuple-element.390), channel_id=1, source_target_pairs={{8,0},{16,8},{24,16},{0,24},{9,1},{17,9},{25,17},{1,25},{10,2},{18... | collective-permute-start | bytes 393224 | tf_op jit(solution)/shard_map/ppermute | solution.py:24
  147.2 13.7 %collective-permute-start.20 = (bf16[128,512]{1,0:T(8,128)(2,1)S(1)}, bf16[128,512]{1,0:T(8,128)(2,1)S(1)}, u32[]{:S(2)}, u32[]{:S(2)}) collective-permute-start(bf16[128,512]{1,0:T(8,128)(2,1)S(1)} %get-tuple-element.389), channel_id=1, source_target_pairs={{24,0},{0,8},{8,16},{16,24},{25,1},{1,9},{9,17},{17,25},{26,2},{2,... | collective-permute-start | bytes 393224 | tf_op jit(solution)/shard_map/ppermute | solution.py:24
  149.6 14.5 %collective-permute-start.24 = (bf16[128,512]{1,0:T(8,128)(2,1)S(1)}, bf16[128,512]{1,0:T(8,128)(2,1)S(1)}, u32[]{:S(2)}, u32[]{:S(2)}) collective-permute-start(bf16[128,512]{1,0:T(8,128)(2,1)S(1)} %get-tuple-element.393), channel_id=1, source_target_pairs={{0,1},{1,2},{2,3},{3,4},{4,5},{5,6},{6,7},{8,9},{9,10},{10,11},{11... | collective-permute-start | bytes 393224 | tf_op jit(solution)/shard_map/ppermute | solution.py:30
  151.5 14.5 %collective-permute-start.25 = (bf16[128,512]{1,0:T(8,128)(2,1)S(1)}, bf16[128,512]{1,0:T(8,128)(2,1)S(1)}, u32[]{:S(2)}, u32[]{:S(2)}) collective-permute-start(bf16[128,512]{1,0:T(8,128)(2,1)S(1)} %get-tuple-element.394), channel_id=1, source_target_pairs={{1,0},{2,1},{3,2},{4,3},{5,4},{6,5},{7,6},{9,8},{10,9},{11,10},{12... | collective-permute-start | bytes 393224 | tf_op jit(solution)/shard_map/ppermute | solution.py:30
  155.8 11.1 %collective-permute-start.3 = (bf16[128,512]{1,0:T(8,128)(2,1)S(1)}, bf16[128,512]{1,0:T(8,128)(2,1)S(1)}, u32[]{:S(2)}, u32[]{:S(2)}) collective-permute-start(bf16[128,512]{1,0:T(8,128)(2,1)S(1)} %collective-permute-done.2), channel_id=1, source_target_pairs={{1,0},{2,1},{3,2},{4,3},{5,4},{6,5},{7,6},{9,8},{10,9},{11,10},{12... | collective-permute-start | bytes 393224 | tf_op jit(solution)/shard_map/ppermute | solution.py:30
  158.5 8.4 %collective-permute-start.1 = (bf16[128,512]{1,0:T(8,128)(2,1)S(1)}, bf16[128,512]{1,0:T(8,128)(2,1)S(1)}, u32[]{:S(2)}, u32[]{:S(2)}) collective-permute-start(bf16[128,512]{1,0:T(8,128)(2,1)S(1)} %collective-permute-done), channel_id=1, source_target_pairs={{0,1},{1,2},{2,3},{3,4},{4,5},{5,6},{6,7},{8,9},{9,10},{10,11},{11... | collective-permute-start | bytes 393224 | tf_op jit(solution)/shard_map/ppermute | solution.py:30
  160.9 6.0 %collective-permute-start.23 = (bf16[128,512]{1,0:T(8,128)(2,1)S(1)}, bf16[128,512]{1,0:T(8,128)(2,1)S(1)}, u32[]{:S(2)}, u32[]{:S(2)}) collective-permute-start(bf16[128,512]{1,0:T(8,128)(2,1)S(1)} %collective-permute-done.22), channel_id=1, source_target_pairs={{1,0},{2,1},{3,2},{4,3},{5,4},{6,5},{7,6},{9,8},{10,9},{11,10},{12... | collective-permute-start | bytes 393224 | tf_op jit(solution)/shard_map/ppermute | solution.py:30
  164.1 6.3 %collective-permute-start.21 = (bf16[128,512]{1,0:T(8,128)(2,1)S(1)}, bf16[128,512]{1,0:T(8,128)(2,1)S(1)}, u32[]{:S(2)}, u32[]{:S(2)}) collective-permute-start(bf16[128,512]{1,0:T(8,128)(2,1)S(1)} %collective-permute-done.20), channel_id=1, source_target_pairs={{0,1},{1,2},{2,3},{3,4},{4,5},{5,6},{6,7},{8,9},{9,10},{10,11},{11... | collective-permute-start | bytes 393224 | tf_op jit(solution)/shard_map/ppermute | solution.py:30
where the time goes:
time: 265 us; the launch traced here: 263 us
  local copies, waits for them, and re-layouts  76.3 us (29%)
  starting transfers between devices  69 us (26%)
  blocking collectives  46.3 us (17%)
  waiting for transfers between devices  30.3 us (11%)
  matrix products  17.2 us (6%)
  other arithmetic  17 us (6%)
  loops' own time  6.22 us (2%)
    ppermute x36, starting transfers between devices, shifted_2(): lax.ppermute(value, axis, [(source, source + steps) for source in range(f...  63.2 us
    ppermute x36, waiting for transfers between devices, shifted_2(): lax.ppermute(value, axis, [(source, source + steps) for source in range(f...  30.3 us
    unnamed x34, local copies, waits for them, and re-layouts  17 us
    all_gather x1, blocking collectives, local(): lax.all_gather(pool_level(second_k), 'outer', axis=0, tiled=True)  15.1 us
    all_gather x1, blocking collectives, local(): lax.all_gather(pool_level(second_v), 'outer', axis=0, tiled=True)  14.1 us
    reshape x4, local copies, waits for them, and re-layouts, attend_block(): head_keys = key_set.reshape(-1, KVHEADS, HD).transpose(1, 0, 2)  13.7 us
    dynamic_slice x12, local copies, waits for them, and re-layouts, one_block(): key_parts.append(lax.dynamic_slice_in_dim(level_k, start_row, 3 * BLOCK, 0))  12.3 us
    dynamic_slice x12, local copies, waits for them, and re-layouts, one_block(): lax.dynamic_slice_in_dim(level_v, start_row, 3 * BLOCK, 0)  12.3 us
  transfers between devices with their start and end apart: 40, of which 7 were waited for; matrix products, arithmetic and copies ran while one was open for 9% of the time, Pallas kernels for 0%

commit v1 on v0

v1 whole, which is shorter than its diff:
```python
import functools
import math

import jax
import jax.numpy as jnp
from jax import lax
from jax.experimental import pallas as pl
from jax.experimental.pallas import tpu as pltpu
from jax.sharding import PartitionSpec as P

HD = 128
QHEADS = 16
KVHEADS = 4
GROUP = QHEADS // KVHEADS
BLOCK = 128
POOL = 8
WIDTH = KVHEADS * HD
BF16 = jnp.bfloat16
F32 = jnp.float32


def pool_rows(rows):
    count = rows.shape[0]
    out_rows = count // POOL
    row = lax.broadcasted_iota(jnp.int32, (out_rows, count), 0)
    column = lax.broadcasted_iota(jnp.int32, (out_rows, count), 1)
    first = row * POOL
    picks = ((column >= first) & (column < first + POOL)).astype(BF16)
    summed = jnp.dot(picks, rows, preferred_element_type=F32)
    return (summed * POOL ** (-0.5)).astype(BF16)


def fused(n_seq, n_outer, has_top, *refs):
    if has_top:
        q_hbm, k_hbm, v_hbm, top_hbm, o_ref = refs[:5]
        scratch = refs[5:]
    else:
        q_hbm, k_hbm, v_hbm, o_ref = refs[:4]
        top_hbm = None
        scratch = refs[4:]
    (q_ref, kv0, kv1, kv2, kv2f, top, peak, acc, load_sem, halo_send, halo_recv, send1, recv1, send2, recv2) = scratch
    tok = q_ref.shape[0]
    blocks = tok // BLOCK
    n = n_seq * n_outer
    me = lax.axis_index("outer") * n_seq + lax.axis_index("seq")

    def peer(t):
        return {"outer": lax.div(t, n_seq), "seq": lax.rem(t, n_seq)}

    def window(level):
        rows = tok // POOL**level
        span = BLOCK // rows
        held = min(3 * span, n)
        def start(t):
            return jnp.clip((lax.div(t, span) - 1) * span, 0, n - held)
        centre = lax.div(me, span)
        low = jnp.maximum((centre - 1) * span, 0)
        high = jnp.minimum((centre + 2) * span, n)
        return rows, span, held, start, low, high

    rows1, span1, held1, start1, low1, high1 = window(1)
    rows2, span2, held2, start2, low2, high2 = window(2)
    base1, base2 = start1(me), start2(me)

    loads = [
        pltpu.make_async_copy(k_hbm, kv0.at[pl.ds(BLOCK, tok), pl.ds(0, WIDTH)], load_sem.at[0]),
        pltpu.make_async_copy(v_hbm, kv0.at[pl.ds(BLOCK, tok), pl.ds(WIDTH, WIDTH)], load_sem.at[1]),
        pltpu.make_async_copy(q_hbm, q_ref, load_sem.at[2]),
    ]
    if has_top:
        loads.append(pltpu.make_async_copy(top_hbm, top, load_sem.at[3]))
    for load in loads:
        load.start()

    barrier = pltpu.get_barrier_semaphore()

    @pl.loop(0, held2)
    def _(j):
        t = base2 + j

        @pl.when((t >= low2) & (t < high2) & (t != me))
        def _():
            pl.semaphore_signal(barrier, inc=1, device_id=peer(t), device_id_type=pl.DeviceIdType.MESH)

    loads[0].wait()
    loads[1].wait()
    pooled1 = pool_rows(kv0[pl.ds(BLOCK, tok), :])
    pooled2 = pool_rows(pooled1)
    kv1[me - base1] = pooled1
    kv2[me - base2] = pooled2
    pl.semaphore_wait(barrier, high2 - low2 - 1)

    def remote(src, dst, send, recv, t):
        return pltpu.make_async_remote_copy(
            src_ref=src, dst_ref=dst, send_sem=send, recv_sem=recv,
            device_id=peer(t), device_id_type=pl.DeviceIdType.MESH,
        )

    def to_upper():
        return remote(kv0.at[pl.ds(tok, BLOCK)], kv0.at[pl.ds(0, BLOCK)], halo_send.at[0], halo_recv.at[0], me + 1)

    def to_lower():
        return remote(
            kv0.at[pl.ds(BLOCK, BLOCK)], kv0.at[pl.ds(BLOCK + tok, BLOCK)], halo_send.at[1], halo_recv.at[1], me - 1
        )

    @pl.when(me + 1 < n)
    def _():
        to_upper().start()

    @pl.when(me > 0)
    def _():
        to_lower().start()

    def level_copy(buffer, start, send, recv, t, base):
        slot = me - start(t)
        return remote(buffer.at[me - base], buffer.at[slot], send.at[t - base], recv.at[slot], t)

    def level_wait(buffer, send, recv, j, t):
        return remote(buffer.at[j], buffer.at[j], send.at[j], recv.at[j], t)

    def send_level(buffer, start, send, recv, base, held, low, high):
        @pl.loop(0, held)
        def _(j):
            t = base + j

            @pl.when((t >= low) & (t < high) & (t != me))
            def _():
                level_copy(buffer, start, send, recv, t, base).start()

    def recv_level(buffer, send, recv, base, held, low, high):
        @pl.loop(0, held)
        def _(j):
            t = base + j

            @pl.when((t >= low) & (t < high) & (t != me))
            def _():
                level_wait(buffer, send, recv, j, t).wait_recv()

    def sent_level(buffer, send, recv, base, held, low, high):
        @pl.loop(0, held)
        def _(j):
            t = base + j

            @pl.when((t >= low) & (t < high) & (t != me))
            def _():
                level_wait(buffer, send, recv, j, t).wait_send()

    send_level(kv1, start1, send1, recv1, base1, held1, low1, high1)
    send_level(kv2, start2, send2, recv2, base2, held2, low2, high2)

    def fill_level(buffer, own, base, held, low, high):
        blank = jnp.concatenate([own[:, :WIDTH], jnp.zeros_like(own[:, WIDTH:])], axis=1)

        @pl.loop(0, held)
        def _(j):
            t = base + j

            @pl.when((t < low) | (t >= high))
            def _():
                buffer[j] = blank

    if n > 2 * span1:
        fill_level(kv1, pooled1, base1, held1, low1, high1)
    if n > 2 * span2:
        fill_level(kv2, pooled2, base2, held2, low2, high2)

    @pl.when(me == 0)
    def _():
        kv0[pl.ds(0, BLOCK), pl.ds(0, WIDTH)] = kv0[pl.ds(BLOCK, BLOCK), pl.ds(0, WIDTH)]
        kv0[pl.ds(0, BLOCK), pl.ds(WIDTH, WIDTH)] = jnp.zeros((BLOCK, WIDTH), BF16)

    @pl.when(me == n - 1)
    def _():
        kv0[pl.ds(BLOCK + tok, BLOCK), pl.ds(0, WIDTH)] = kv0[pl.ds(tok, BLOCK), pl.ds(0, WIDTH)]
        kv0[pl.ds(BLOCK + tok, BLOCK), pl.ds(WIDTH, WIDTH)] = jnp.zeros((BLOCK, WIDTH), BF16)

    loads[2].wait()
    scale = HD ** (-0.5) * math.log2(math.e)

    def query(h, b):
        parts = []
        for g in range(GROUP):
            column = pl.multiple_of(h * (GROUP * HD) + g * HD, HD)
            parts.append(q_ref[pl.ds(b * BLOCK, BLOCK), pl.ds(column, HD)])
        return jnp.concatenate(parts, axis=0)

    def scored(h, b, parts, first, last):
        q = query(h, b)
        unit = h * blocks + b
        scores = [
            lax.dot_general(q, k, (((1,), (1,)), ((), ())), preferred_element_type=F32) for k, _ in parts
        ]
        highest = jnp.max(scores[0], axis=1, keepdims=True)
        for s in scores[1:]:
            highest = jnp.maximum(highest, jnp.max(s, axis=1, keepdims=True))
        if not first:
            old = peak[unit][:, :1]
            highest = jnp.maximum(highest, old)
        mixed = None
        for s, (_, v) in zip(scores, parts):
            weights = jnp.exp2((s - highest) * scale).astype(BF16)
            term = jnp.dot(weights, v, preferred_element_type=F32)
            mixed = term if mixed is None else mixed + term
        if not first:
            mixed = mixed + acc[unit] * jnp.exp2((old - highest) * scale)
        if not last:
            peak[unit] = jnp.broadcast_to(highest, (GROUP * BLOCK, HD))
            acc[unit] = mixed
            return
        out = (mixed[:, :HD] / mixed[:, HD:]).astype(BF16)
        for g in range(GROUP):
            column = pl.multiple_of(h * (GROUP * HD) + g * HD, HD)
            o_ref[pl.ds(b * BLOCK, BLOCK), pl.ds(column, HD)] = out[g * BLOCK : (g + 1) * BLOCK]

    def head_columns(h):
        return pl.multiple_of(h * HD, HD), pl.multiple_of(WIDTH + h * HD, HD)

    def with_count(v, count):
        return jnp.concatenate([v, count], axis=1)

    def counts(rows, low, high):
        row = lax.broadcasted_iota(jnp.int32, (rows, HD), 0)
        return ((row >= low) & (row < high)).astype(F32).astype(BF16)

    def fine(h, start, size, present):
        key_column, value_column = head_columns(h)
        k = kv0[pl.ds(start, size), pl.ds(key_column, HD)]
        v = kv0[pl.ds(start, size), pl.ds(value_column, HD)]
        count = jnp.ones((size, HD), BF16) if present is None else counts(size, 0, jnp.where(present, size, 0))
        return k, with_count(v, count)

    @pl.loop(0, KVHEADS)
    def _(h):
        for b in range(blocks):
            low, high = max(b, 1), min(b + 2, blocks)
            scored(h, b, [fine(h, low * BLOCK, (high - low + 1) * BLOCK, None)], True, False)

    @pl.when(me > 0)
    def _():
        to_upper().wait_recv()

    @pl.when(me + 1 < n)
    def _():
        to_lower().wait_recv()

    recv_level(kv1, send1, recv1, base1, held1, low1, high1)

    @pl.loop(0, KVHEADS)
    def _(h):
        key_column, value_column = head_columns(h)
        k1 = kv1[:, :, pl.ds(key_column, HD)].reshape(held1 * rows1, HD)
        v1 = kv1[:, :, pl.ds(value_column, HD)].reshape(held1 * rows1, HD)
        coarse = (k1, with_count(v1, counts(held1 * rows1, (low1 - base1) * rows1, (high1 - base1) * rows1)))
        for b in range(blocks):
            parts = [coarse]
            if b == 0:
                parts.append(fine(h, 0, BLOCK, me > 0))
            if b == blocks - 1:
                parts.append(fine(h, BLOCK + tok, BLOCK, me < n - 1))
            scored(h, b, parts, False, False)

    recv_level(kv2, send2, recv2, base2, held2, low2, high2)
    kv2f[...] = kv2[...].astype(F32).reshape(held2 * rows2, 2 * WIDTH).astype(BF16)
    if not has_top:
        top[...] = pool_rows(kv2f[...])
    else:
        loads[3].wait()

    @pl.loop(0, KVHEADS)
    def _(h):
        key_column, value_column = head_columns(h)
        k2 = kv2f[:, pl.ds(key_column, HD)]
        v2 = kv2f[:, pl.ds(value_column, HD)]
        count2 = counts(held2 * rows2, (low2 - base2) * rows2, (high2 - base2) * rows2)
        k3 = top[:, pl.ds(key_column, HD)]
        v3 = top[:, pl.ds(value_column, HD)]
        parts = [(k2, with_count(v2, count2)), (k3, with_count(v3, jnp.ones((v3.shape[0], HD), BF16)))]
        for b in range(blocks):
            scored(h, b, parts, False, True)

    @pl.when(me + 1 < n)
    def _():
        to_upper().wait_send()

    @pl.when(me > 0)
    def _():
        to_lower().wait_send()

    sent_level(kv1, send1, recv1, base1, held1, low1, high1)
    sent_level(kv2, send2, recv2, base2, held2, low2, high2)


def pool_level(rows):
    summed = rows.astype(F32).reshape(rows.shape[0] // POOL, POOL, rows.shape[1]).sum(axis=1)
    return (summed * POOL ** (-0.5)).astype(BF16)


def local(n_seq, n_outer, queries, keys, values):
    tok = queries.shape[0]
    n = n_seq * n_outer
    rows1, rows2 = tok // POOL, tok // POOL**2
    held1 = min(3 * (BLOCK // rows1), n)
    held2 = min(3 * (BLOCK // rows2), n)
    has_top = held2 < n
    operands = [queries, keys, values]
    if has_top:
        joined = jnp.concatenate([keys, values], axis=1)
        own = pool_level(pool_level(pool_level(joined)))
        operands.append(lax.all_gather(own, ("outer", "seq"), axis=0, tiled=True))
    top_rows = n * tok // POOL**3
    units = KVHEADS * (tok // BLOCK)
    return pl.pallas_call(
        functools.partial(fused, n_seq, n_outer, has_top),
        out_shape=jax.ShapeDtypeStruct((tok, QHEADS * HD), BF16),
        in_specs=[pl.BlockSpec(memory_space=pl.ANY)] * len(operands),
        out_specs=pl.BlockSpec(memory_space=pltpu.VMEM),
        scratch_shapes=[
            pltpu.VMEM((tok, QHEADS * HD), BF16),
            pltpu.VMEM((tok + 2 * BLOCK, 2 * WIDTH), BF16),
            pltpu.VMEM((held1, rows1, 2 * WIDTH), BF16),
            pltpu.VMEM((held2, rows2, 2 * WIDTH), BF16),
            pltpu.VMEM((held2 * rows2, 2 * WIDTH), BF16),
            pltpu.VMEM((top_rows, 2 * WIDTH), BF16),
            pltpu.VMEM((units, GROUP * BLOCK, HD), F32),
            pltpu.VMEM((units, GROUP * BLOCK, 2 * HD), F32),
            pltpu.SemaphoreType.DMA((4,)),
            pltpu.SemaphoreType.DMA((2,)),
            pltpu.SemaphoreType.DMA((2,)),
            pltpu.SemaphoreType.DMA((held1,)),
            pltpu.SemaphoreType.DMA((held1,)),
            pltpu.SemaphoreType.DMA((held2,)),
            pltpu.SemaphoreType.DMA((held2,)),
        ],
        compiler_params=pltpu.CompilerParams(
            collective_id=0, has_side_effects=True, vmem_limit_bytes=56 * 1024 * 1024
        ),
    )(*operands)


def solution(mesh):
    spec = P(("outer", "seq"), None)
    return jax.shard_map(
        functools.partial(local, mesh.shape["seq"], mesh.shape["outer"]),
        mesh=mesh,
        in_specs=(spec, spec, spec),
        out_specs=spec,
        check_vma=False,
    )
```

time: 265 us -> 60 us (0.23)
  the two profiles are of different devices: /device:TPU:26 before, /device:TPU:5 now
where the time goes in v1:
time: 60 us; the launch traced here: 59.9 us
  Pallas kernels  56.7 us (94%)
  local copies, waits for them, and re-layouts  3.16 us (5%)
    pallas_call x1, Pallas kernels, local(): pl.pallas_call(functools.partial(fused, n_seq, n_outer, has_top), out_sha...  56.7 us
    unnamed x1, local copies, waits for them, and re-layouts  3.16 us

profile of v1, /device:TPU:5, one launch (start us, length us, event | category | flops | bytes accessed | tf_op | source)
XLA Modules:
  0.0 59.9 jit_solution(2132642992007962461)
XLA Ops:
  0.0 56.7 %shard_map.37 = bf16[512,2048]{1,0:T(8,128)(2,1)} custom-call(bf16[512,2048]{1,0:T(8,128)(2,1)} %refs_0_.1, bf16[512,512]{1,0:T(8,128)(2,1)} %refs_1_.1, bf16[512,512]{1,0:T(8,128)(2,1)} %refs_2_.1), custom_call_target="tpu_custom_call" | custom-call | tf_op jit(solution)/shard_map/pallas_call | solution.py:313
  56.7 3.2 %copy.5 = bf16[512,2048]{1,0:T(8,128)(2,1)} copy(bf16[512,2048]{1,0:T(8,128)(2,1)} %shard_map.37) | data formatting | bytes 4194304

commit v2 on v1

v2 whole, which is shorter than its diff:
```python
import functools
import math

import jax
import jax.numpy as jnp
from jax import lax
from jax.experimental import pallas as pl
from jax.experimental.pallas import tpu as pltpu
from jax.sharding import PartitionSpec as P

HD = 128
QHEADS = 16
KVHEADS = 4
GROUP = QHEADS // KVHEADS
BLOCK = 128
POOL = 8
WIDTH = KVHEADS * HD
BF16 = jnp.bfloat16
F32 = jnp.float32


def pool_rows(rows):
    count = rows.shape[0]
    out_rows = count // POOL
    row = lax.broadcasted_iota(jnp.int32, (out_rows, count), 0)
    column = lax.broadcasted_iota(jnp.int32, (out_rows, count), 1)
    first = row * POOL
    picks = ((column >= first) & (column < first + POOL)).astype(BF16)
    summed = jnp.dot(picks, rows, preferred_element_type=F32)
    return (summed * POOL ** (-0.5)).astype(BF16)


def fused(n_seq, n_outer, spread, *refs):
    if spread:
        q_hbm, k_hbm, v_hbm, o_ref = refs[:4]
        top_hbm = None
        scratch = refs[4:]
    else:
        q_hbm, k_hbm, v_hbm, top_hbm, o_ref = refs[:5]
        scratch = refs[5:]
    (q_ref, kv0, kvc, kv2, peak, acc, load_sem, halo_send, halo_recv, send1, recv1, send2, recv2) = scratch
    tok = q_ref.shape[0]
    blocks = tok // BLOCK
    n = n_seq * n_outer
    rows1, rows2 = tok // POOL, tok // POOL**2
    span2 = BLOCK // rows2
    held2 = kv2.shape[0] * kv2.shape[1]
    pair = 2 * rows1
    level1 = 3 * BLOCK
    level2 = held2 * rows2
    top_rows = n * tok // POOL**3
    me = lax.axis_index("outer") * n_seq + lax.axis_index("seq")
    odd = lax.rem(me, 2)
    last_pair = n // 2 - 1
    a = lax.div(me, 2)
    phase = lax.rem(a, 4)
    a_odd = lax.rem(a, 2)

    def peer(t):
        return {"outer": lax.div(t, n_seq), "seq": lax.rem(t, n_seq)}

    def flipped(bit):
        return me + bit - 2 * bit * lax.rem(lax.div(me, bit), 2)

    def remote(src, dst, send, recv, t):
        return pltpu.make_async_remote_copy(
            src_ref=src, dst_ref=dst, send_sem=send, recv_sem=recv,
            device_id=peer(t), device_id_type=pl.DeviceIdType.MESH,
        )

    centre2 = lax.div(me, span2)
    low2 = jnp.maximum((centre2 - 1) * span2, 0)
    high2 = jnp.minimum((centre2 + 2) * span2, n)

    def start2(t):
        return jnp.clip((lax.div(t, span2) - 1) * span2, 0, n - held2)

    base2 = start2(me)

    loads = [
        pltpu.make_async_copy(k_hbm, kv0.at[pl.ds(BLOCK, tok), pl.ds(0, WIDTH)], load_sem.at[0]),
        pltpu.make_async_copy(v_hbm, kv0.at[pl.ds(BLOCK, tok), pl.ds(WIDTH, WIDTH)], load_sem.at[1]),
        pltpu.make_async_copy(q_hbm, q_ref, load_sem.at[2]),
    ]
    top_at = level1 + level2
    if not spread:
        loads.append(pltpu.make_async_copy(top_hbm, kvc.at[pl.ds(top_at, top_rows)], load_sem.at[3]))
    for load in loads:
        load.start()

    across = me - 1 + 2 * odd
    has_across = (across >= 0) & (across < n)
    cross_up = (phase == 3) & (a < last_pair)
    cross_down = (phase == 0) & (a > 0)

    barrier = pltpu.get_barrier_semaphore()

    def greet(t):
        pl.semaphore_signal(barrier, inc=1, device_id=peer(t), device_id_type=pl.DeviceIdType.MESH)

    if spread:
        bits = []
        bit = POOL
        while bit < n:
            bits.append(bit)
            bit *= 2
        bits += [1, 2, 4]
        for bit in bits:
            greet(flipped(bit))
        pl.when(has_across)(lambda: greet(across))
        pl.when(cross_up)(lambda: greet(me + 2))
        pl.when(cross_down)(lambda: greet(me - 2))
        met = len(bits) + has_across.astype(jnp.int32) + (cross_up | cross_down).astype(jnp.int32)
    else:
        @pl.loop(0, held2)
        def _(j):
            t = base2 + j
            pl.when((t >= low2) & (t < high2) & (t != me))(lambda: greet(t))

        met = high2 - low2 - 1

    loads[0].wait()
    loads[1].wait()
    pooled1 = pool_rows(kv0[pl.ds(BLOCK, tok), :])
    own1 = pl.multiple_of(pair + odd * rows1, rows1)
    kvc[pl.ds(own1, rows1), :] = pooled1
    pooled2 = pool_rows(pooled1)
    slot = me - base2
    kv2[lax.div(slot, POOL), lax.rem(slot, POOL)] = pooled2
    pl.semaphore_wait(barrier, met)

    def pair_at(start):
        return kvc.at[pl.ds(pl.multiple_of(start, pair), pair)]

    def half_copy():
        rows = kvc.at[pl.ds(own1, rows1)]
        return remote(rows, rows, send1.at[0], recv1.at[0], flipped(1))

    def half_wait():
        rows = kvc.at[pl.ds(pl.multiple_of(pair + (1 - odd) * rows1, rows1), rows1)]
        return remote(rows, rows, send1.at[0], recv1.at[0], flipped(1))

    def swap_copy():
        return remote(pair_at(pair), pair_at(a_odd * (2 * pair)), send1.at[1], recv1.at[1], flipped(2))

    def swap_wait():
        rows = pair_at((1 - a_odd) * (2 * pair))
        return remote(rows, rows, send1.at[1], recv1.at[1], flipped(2))

    def cross_copy(up):
        return remote(
            pair_at(pair), pair_at(0 if up else 2 * pair), send1.at[2], recv1.at[2], me + 2 if up else me - 2
        )

    def pass_copy(up):
        return remote(
            pair_at(2 * pair if up else 0), pair_at(0 if up else 2 * pair), send1.at[3], recv1.at[2],
            me + 4 if up else me - 4,
        )

    def third_wait():
        rows = pair_at(a_odd * (2 * pair))
        return remote(rows, rows, send1.at[2], recv1.at[2], flipped(4))

    has_third = (phase == 1) | (phase == 2) | cross_up | cross_down

    def halo_copy(up):
        if up:
            return remote(kv0.at[pl.ds(tok, BLOCK)], kv0.at[pl.ds(0, BLOCK)], halo_send.at[0], halo_recv.at[0], me + 1)
        return remote(
            kv0.at[pl.ds(BLOCK, BLOCK)], kv0.at[pl.ds(BLOCK + tok, BLOCK)], halo_send.at[1], halo_recv.at[1], me - 1
        )

    def halo_start(wanted):
        pl.when((me + 1 < n) & (odd == (1 - wanted)))(lambda: halo_copy(True).start())
        pl.when((me > 0) & (odd == wanted))(lambda: halo_copy(False).start())

    if spread:
        def region(step, whose):
            bit = bits[step]
            flips = lax.rem(lax.div(me, bit), 2)
            at = me if whose == 0 else me + bit - 2 * bit * flips
            k, l = lax.div(at, POOL), lax.rem(at, POOL)
            if bit >= POOL:
                size = bit // POOL
                return kv2.at[pl.ds(lax.div(k, size) * size, size), pl.ds(l, 1)]
            return kv2.at[:, pl.ds(lax.div(l, bit) * bit, bit)]

        def step_copy(step):
            rows = region(step, 0)
            return remote(rows, rows, send2.at[step], recv2.at[step], flipped(bits[step]))

        def step_wait(step):
            rows = region(step, 1)
            return remote(rows, rows, send2.at[step], recv2.at[step], flipped(bits[step]))
    else:
        def over_window(act):
            @pl.loop(0, held2)
            def _(j):
                t = base2 + j
                pl.when((t >= low2) & (t < high2) & (t != me))(lambda: act(j, t))

        def slot_at(j):
            return kv2.at[lax.div(j, POOL), lax.rem(j, POOL)]

        def direct_copy(j, t):
            there = me - start2(t)
            remote(slot_at(slot), slot_at(there), send2.at[j], recv2.at[there], t).start()

        def direct_wait(j, t):
            return remote(slot_at(j), slot_at(j), send2.at[j], recv2.at[j], t)

    half_copy().start()
    if spread:
        step_copy(0).start()

    def blank_of(own):
        return jnp.concatenate([own[:, :WIDTH], jnp.zeros_like(own[:, WIDTH:])], axis=1)

    blank1 = jnp.concatenate([blank_of(pooled1)] * 2, axis=0)

    @pl.when(a == 0)
    def _():
        kvc[pl.ds(0, pair), :] = blank1

    @pl.when(a == last_pair)
    def _():
        kvc[pl.ds(2 * pair, pair), :] = blank1

    if n > 2 * span2:
        blank2 = blank_of(pooled2)

        @pl.loop(0, held2)
        def _(j):
            t = base2 + j

            @pl.when((t < low2) | (t >= high2))
            def _():
                kv2[lax.div(j, POOL), lax.rem(j, POOL)] = blank2

    @pl.when(me == 0)
    def _():
        kv0[pl.ds(0, BLOCK), :] = blank_of(kv0[pl.ds(BLOCK, BLOCK), :])

    @pl.when(me == n - 1)
    def _():
        kv0[pl.ds(BLOCK + tok, BLOCK), :] = blank_of(kv0[pl.ds(tok, BLOCK), :])

    loads[2].wait()
    scale = HD ** (-0.5) * math.log2(math.e)

    def query(h, b):
        parts = []
        for g in range(GROUP):
            column = pl.multiple_of(h * (GROUP * HD) + g * HD, HD)
            parts.append(q_ref[pl.ds(b * BLOCK, BLOCK), pl.ds(column, HD)])
        return jnp.concatenate(parts, axis=0)

    def across_lanes(x, width):
        if width % HD == 0:
            return jnp.concatenate([x] * (width // HD), axis=1)
        whole = [x] * (width // HD) + [x[:, : width % HD]]
        return jnp.concatenate(whole, axis=1)

    def scored(h, b, k, v, first, last):
        q = query(h, b)
        unit = h * blocks + b
        s = lax.dot_general(q, k, (((1,), (1,)), ((), ())), preferred_element_type=F32)
        highest = jnp.broadcast_to(jnp.max(s, axis=1, keepdims=True), (GROUP * BLOCK, HD))
        if not first:
            old = peak[unit]
            highest = jnp.maximum(highest, old)
        weights = jnp.exp2((s - across_lanes(highest, s.shape[1])) * scale).astype(BF16)
        mixed = jnp.dot(weights, v, preferred_element_type=F32)
        if not first:
            keep = jnp.exp2((old - highest) * scale)
            mixed = mixed + acc[unit] * across_lanes(keep, 2 * HD)
        if not last:
            peak[unit] = highest
            acc[unit] = mixed
            return
        out = (mixed[:, :HD] / mixed[:, HD:]).astype(BF16)
        for g in range(GROUP):
            column = pl.multiple_of(h * (GROUP * HD) + g * HD, HD)
            o_ref[pl.ds(b * BLOCK, BLOCK), pl.ds(column, HD)] = out[g * BLOCK : (g + 1) * BLOCK]

    def head_columns(h):
        return pl.multiple_of(h * HD, HD), pl.multiple_of(WIDTH + h * HD, HD)

    def fine(h, start, size, present):
        key_column, value_column = head_columns(h)
        k = kv0[pl.ds(start, size), pl.ds(key_column, HD)]
        v = kv0[pl.ds(start, size), pl.ds(value_column, HD)]
        if present is None:
            count = jnp.ones((size, HD), BF16)
        else:
            row = lax.broadcasted_iota(jnp.int32, (size, HD), 0)
            count = (row < jnp.where(present, size, 0)).astype(F32).astype(BF16)
        return k, jnp.concatenate([v, count], axis=1)

    def own_rows(h):
        for b in range(blocks):
            low, high = max(b, 1), min(b + 2, blocks)
            scored(h, b, *fine(h, low * BLOCK, (high - low + 1) * BLOCK, None), True, False)

    def own_loop(low, high):
        @pl.loop(low, high)
        def _(h):
            own_rows(h)

    if spread:
        zs = len(bits) - 3
        at = 0
        for z in range(zs):
            stop = at + 1 if at < KVHEADS else at
            own_loop(at, stop)
            at = stop
            step_wait(z).wait_recv()
            step_copy(z + 1).start()
        half_wait().wait_recv()
        swap_copy().start()
        pl.when(cross_up)(lambda: cross_copy(True).start())
        pl.when(cross_down)(lambda: cross_copy(False).start())
        halo_start(1)
        stop = max(at, KVHEADS - 1)
        own_loop(at, stop)
        step_wait(zs).wait_recv()
        step_copy(zs + 1).start()
        halo_start(0)
        own_loop(stop, KVHEADS)
    else:
        over_window(direct_copy)
        half_wait().wait_recv()
        swap_copy().start()
        pl.when(cross_up)(lambda: cross_copy(True).start())
        pl.when(cross_down)(lambda: cross_copy(False).start())
        halo_start(1)
        halo_start(0)
        own_loop(0, KVHEADS)

    swap_wait().wait_recv()
    pl.when(phase == 0)(lambda: pass_copy(True).start())
    pl.when(phase == 3)(lambda: pass_copy(False).start())
    if spread:
        step_wait(zs + 1).wait_recv()
        step_copy(zs + 2).start()
        step_wait(zs + 2).wait_recv()
    else:
        over_window(lambda j, t: direct_wait(j, t).wait_recv())
    second = kv2[...].astype(F32).reshape(level2, 2 * WIDTH).astype(BF16)
    kvc[pl.ds(level1, level2), :] = second
    if spread:
        kvc[pl.ds(top_at, top_rows), :] = pool_rows(second)
    else:
        loads[3].wait()
    pl.when(has_third)(lambda: third_wait().wait_recv())

    coarse_rows = level1 + level2 + top_rows
    row = lax.broadcasted_iota(jnp.int32, (coarse_rows, HD), 0)
    missing = ((row < jnp.where(a == 0, pair, 0))) | (
        (row >= jnp.where(a == last_pair, 2 * pair, level1)) & (row < level1)
    )
    if n > 2 * span2:
        missing = missing | (
            (row >= level1) & (row < top_at)
            & ((row < level1 + (low2 - base2) * rows2) | (row >= level1 + (high2 - base2) * rows2))
        )
    coarse_count = jnp.where(missing, 0.0, 1.0).astype(BF16)

    @pl.loop(0, KVHEADS)
    def _(h):
        key_column, value_column = head_columns(h)
        k = kvc[:, pl.ds(key_column, HD)]
        v = jnp.concatenate([kvc[:, pl.ds(value_column, HD)], coarse_count], axis=1)
        for b in range(blocks):
            scored(h, b, k, v, False, 0 < b < blocks - 1)

    pl.when(me > 0)(lambda: halo_copy(True).wait_recv())
    pl.when(me + 1 < n)(lambda: halo_copy(False).wait_recv())

    @pl.loop(0, KVHEADS)
    def _(h):
        scored(h, 0, *fine(h, 0, BLOCK, me > 0), False, blocks > 1)
        scored(h, blocks - 1, *fine(h, BLOCK + tok, BLOCK, me < n - 1), False, True)

    pl.when(me + 1 < n)(lambda: halo_copy(True).wait_send())
    pl.when(me > 0)(lambda: halo_copy(False).wait_send())
    half_copy().wait_send()
    swap_copy().wait_send()
    pl.when(cross_up)(lambda: cross_copy(True).wait_send())
    pl.when(cross_down)(lambda: cross_copy(False).wait_send())
    pl.when(phase == 0)(lambda: pass_copy(True).wait_send())
    pl.when(phase == 3)(lambda: pass_copy(False).wait_send())
    if spread:
        for step in range(len(bits)):
            step_copy(step).wait_send()
    else:
        over_window(lambda j, t: direct_wait(j, t).wait_send())


def pool_level(rows):
    summed = rows.astype(F32).reshape(rows.shape[0] // POOL, POOL, rows.shape[1]).sum(axis=1)
    return (summed * POOL ** (-0.5)).astype(BF16)


def local(n_seq, n_outer, queries, keys, values):
    tok = queries.shape[0]
    n = n_seq * n_outer
    rows1, rows2 = tok // POOL, tok // POOL**2
    assert 2 * rows1 == BLOCK and n % 8 == 0
    held2 = min(3 * (BLOCK // rows2), n)
    spread = held2 == n and n & (n - 1) == 0
    operands = [queries, keys, values]
    if not spread:
        joined = jnp.concatenate([keys, values], axis=1)
        own = pool_level(pool_level(pool_level(joined)))
        operands.append(lax.all_gather(own, ("outer", "seq"), axis=0, tiled=True))
    coarse_rows = 3 * BLOCK + held2 * rows2 + n * tok // POOL**3
    units = KVHEADS * (tok // BLOCK)
    return pl.pallas_call(
        functools.partial(fused, n_seq, n_outer, spread),
        out_shape=jax.ShapeDtypeStruct((tok, QHEADS * HD), BF16),
        in_specs=[pl.BlockSpec(memory_space=pltpu.HBM)] * len(operands),
        out_specs=pl.BlockSpec(memory_space=pltpu.VMEM),
        scratch_shapes=[
            pltpu.VMEM((tok, QHEADS * HD), BF16),
            pltpu.VMEM((tok + 2 * BLOCK, 2 * WIDTH), BF16),
            pltpu.VMEM((coarse_rows, 2 * WIDTH), BF16),
            pltpu.VMEM((held2 // POOL, POOL, rows2, 2 * WIDTH), BF16),
            pltpu.VMEM((units, GROUP * BLOCK, HD), F32),
            pltpu.VMEM((units, GROUP * BLOCK, 2 * HD), F32),
            pltpu.SemaphoreType.DMA((4,)),
            pltpu.SemaphoreType.DMA((2,)),
            pltpu.SemaphoreType.DMA((2,)),
            pltpu.SemaphoreType.DMA((4,)),
            pltpu.SemaphoreType.DMA((3,)),
            pltpu.SemaphoreType.DMA((held2,)),
            pltpu.SemaphoreType.DMA((held2,)),
        ],
        compiler_params=pltpu.CompilerParams(
            collective_id=0, has_side_effects=True, vmem_limit_bytes=44 * 1024 * 1024
        ),
    )(*operands)


def solution(mesh):
    spec = P(("outer", "seq"), None)
    return jax.shard_map(
        functools.partial(local, mesh.shape["seq"], mesh.shape["outer"]),
        mesh=mesh,
        in_specs=(spec, spec, spec),
        out_specs=spec,
        check_vma=False,
    )
```

time: 60 us -> 49.5 us (0.82)
  Pallas kernels: 56.7 us -> 44.3 us
  local copies, waits for them, and re-layouts: 3.16 us -> 4.99 us
    pallas_call x1, Pallas kernels: 56.7 us -> 44.3 us  [local(): pl.pallas_call(functools.partial(fused, n_seq, n_outer, spread), out_shap...]
    unnamed x1 -> x7, local copies, waits for them, and re-layouts: 3.16 us -> 4.99 us
where the time goes in v2:
time: 49.5 us; the launch traced here: 49.3 us
  Pallas kernels  44.3 us (89%)
  local copies, waits for them, and re-layouts  4.99 us (10%)
    pallas_call x1, Pallas kernels, local(): pl.pallas_call(functools.partial(fused, n_seq, n_outer, spread), out_shap...  44.3 us
    unnamed x7, local copies, waits for them, and re-layouts  4.99 us

profile of v2, /device:TPU:5, one launch (start us, length us, event | category | flops | bytes accessed | tf_op | source)
XLA Modules:
  0.0 49.3 jit_solution(1795277036802014519)
XLA Ops:
  0.0 0.0 copy-start
  0.0 1.6 %copy-done = bf16[512,2048]{1,0:T(8,128)(2,1)S(1)} copy-done((bf16[512,2048]{1,0:T(8,128)(2,1)S(1)}, bf16[512,2048]{1,0:T(8,128)(2,1)}, u32[]{:S(2)}) %copy-start) | copy-done | bytes 2097176
  1.6 0.0 copy-start.1
  1.6 1.0 %copy-done.1 = bf16[512,512]{1,0:T(8,128)(2,1)S(1)} copy-done((bf16[512,512]{1,0:T(8,128)(2,1)S(1)}, bf16[512,512]{1,0:T(8,128)(2,1)}, u32[]{:S(2)}) %copy-start.1) | copy-done | bytes 524312
  2.6 0.0 copy-start.2
  2.6 1.0 %copy-done.2 = bf16[512,512]{1,0:T(8,128)(2,1)S(1)} copy-done((bf16[512,512]{1,0:T(8,128)(2,1)S(1)}, bf16[512,512]{1,0:T(8,128)(2,1)}, u32[]{:S(2)}) %copy-start.2) | copy-done | bytes 524312
  3.7 44.3 %shard_map.37 = bf16[512,2048]{1,0:T(8,128)(2,1)S(1)} custom-call(bf16[512,2048]{1,0:T(8,128)(2,1)S(1)} %copy-done, bf16[512,512]{1,0:T(8,128)(2,1)S(1)} %copy-done.1, bf16[512,512]{1,0:T(8,128)(2,1)S(1)} %copy-done.2), custom_call_target="tpu_custom_call" | custom-call | tf_op jit(solution)/shard_map/pallas_call | solution.py:420
  48.0 1.3 %copy.5 = bf16[512,2048]{1,0:T(8,128)(2,1)} copy(bf16[512,2048]{1,0:T(8,128)(2,1)S(1)} %shard_map.37) | data formatting | bytes 4194304
Async XLA Ops:
  0.0 1.6 %copy-start = (bf16[512,2048]{1,0:T(8,128)(2,1)S(1)}, bf16[512,2048]{1,0:T(8,128)(2,1)}, u32[]{:S(2)}) copy-start(bf16[512,2048]{1,0:T(8,128)(2,1)} %refs_0_.1) | copy-start | bytes 6291460
  1.6 1.0 %copy-start.1 = (bf16[512,512]{1,0:T(8,128)(2,1)S(1)}, bf16[512,512]{1,0:T(8,128)(2,1)}, u32[]{:S(2)}) copy-start(bf16[512,512]{1,0:T(8,128)(2,1)} %refs_1_.1) | copy-start | bytes 1572868
  2.6 1.0 %copy-start.2 = (bf16[512,512]{1,0:T(8,128)(2,1)S(1)}, bf16[512,512]{1,0:T(8,128)(2,1)}, u32[]{:S(2)}) copy-start(bf16[512,512]{1,0:T(8,128)(2,1)} %refs_2_.1) | copy-start | bytes 1572868

commit v3 on v2

--- a/solution.py
+++ b/solution.py
@@ -15,6 +15,9 @@
 BLOCK = 128
 POOL = 8
 WIDTH = KVHEADS * HD
+PER_HEAD = 2 * HD
+CHUNKS = 2
+CHUNK = 2 * WIDTH // CHUNKS
 BF16 = jnp.bfloat16
 F32 = jnp.float32
 
@@ -77,14 +80,21 @@
 
     base2 = start2(me)
 
-    loads = [
-        pltpu.make_async_copy(k_hbm, kv0.at[pl.ds(BLOCK, tok), pl.ds(0, WIDTH)], load_sem.at[0]),
-        pltpu.make_async_copy(v_hbm, kv0.at[pl.ds(BLOCK, tok), pl.ds(WIDTH, WIDTH)], load_sem.at[1]),
-        pltpu.make_async_copy(q_hbm, q_ref, load_sem.at[2]),
-    ]
+    loads = []
+    for h in range(KVHEADS):
+        for part, source in enumerate((k_hbm, v_hbm)):
+            columns = pl.ds(h * PER_HEAD + part * HD, HD)
+            loads.append(
+                pltpu.make_async_copy(
+                    source.at[:, pl.ds(h * HD, HD)], kv0.at[pl.ds(BLOCK, tok), columns], load_sem.at[len(loads)]
+                )
+            )
+    own_loads = list(loads)
+    q_load = pltpu.make_async_copy(q_hbm, q_ref, load_sem.at[2 * KVHEADS])
+    loads.append(q_load)
     top_at = level1 + level2
     if not spread:
-        loads.append(pltpu.make_async_copy(top_hbm, kvc.at[pl.ds(top_at, top_rows)], load_sem.at[3]))
+        loads.append(pltpu.make_async_copy(top_hbm, kvc.at[pl.ds(top_at, top_rows)], load_sem.at[2 * KVHEADS + 1]))
     for load in loads:
         load.start()
 
@@ -104,7 +114,7 @@
         while bit < n:
             bits.append(bit)
             bit *= 2
-        bits += [1, 2, 4]
+        bits += [2, 1, 4]
         for bit in bits:
             greet(flipped(bit))
         pl.when(has_across)(lambda: greet(across))
@@ -119,80 +129,99 @@
 
         met = high2 - low2 - 1
 
-    loads[0].wait()
-    loads[1].wait()
+    for load in own_loads:
+        load.wait()
     pooled1 = pool_rows(kv0[pl.ds(BLOCK, tok), :])
     own1 = pl.multiple_of(pair + odd * rows1, rows1)
     kvc[pl.ds(own1, rows1), :] = pooled1
     pooled2 = pool_rows(pooled1)
     slot = me - base2
-    kv2[lax.div(slot, POOL), lax.rem(slot, POOL)] = pooled2
+
+    def inner(t):
+        low = lax.rem(t, POOL)
+        if not spread:
+            return low
+        return lax.rem(low, 2) * 2 + lax.rem(lax.div(low, 2), 2) + lax.div(low, 4) * 4
+
+    kv2[lax.div(slot, POOL), inner(slot)] = pooled2
     pl.semaphore_wait(barrier, met)
 
-    def pair_at(start):
-        return kvc.at[pl.ds(pl.multiple_of(start, pair), pair)]
-
-    def half_copy():
-        rows = kvc.at[pl.ds(own1, rows1)]
-        return remote(rows, rows, send1.at[0], recv1.at[0], flipped(1))
-
-    def half_wait():
-        rows = kvc.at[pl.ds(pl.multiple_of(pair + (1 - odd) * rows1, rows1), rows1)]
-        return remote(rows, rows, send1.at[0], recv1.at[0], flipped(1))
-
-    def swap_copy():
-        return remote(pair_at(pair), pair_at(a_odd * (2 * pair)), send1.at[1], recv1.at[1], flipped(2))
-
-    def swap_wait():
-        rows = pair_at((1 - a_odd) * (2 * pair))
-        return remote(rows, rows, send1.at[1], recv1.at[1], flipped(2))
-
-    def cross_copy(up):
+    def columns_of(c):
+        return pl.ds(c * CHUNK, CHUNK)
+
+    def pair_at(start, c):
+        return kvc.at[pl.ds(pl.multiple_of(start, pair), pair), columns_of(c)]
+
+    def half_copy(c):
+        rows = kvc.at[pl.ds(own1, rows1), columns_of(c)]
+        return remote(rows, rows, send1.at[c, 0], recv1.at[c, 0], flipped(1))
+
+    def half_wait(c):
+        rows = kvc.at[pl.ds(pl.multiple_of(pair + (1 - odd) * rows1, rows1), rows1), columns_of(c)]
+        return remote(rows, rows, send1.at[c, 0], recv1.at[c, 0], flipped(1))
+
+    def swap_copy(c):
         return remote(
-            pair_at(pair), pair_at(0 if up else 2 * pair), send1.at[2], recv1.at[2], me + 2 if up else me - 2
+            pair_at(pair, c), pair_at(a_odd * (2 * pair), c), send1.at[c, 1], recv1.at[c, 1], flipped(2)
         )
 
-    def pass_copy(up):
+    def swap_wait(c):
+        rows = pair_at((1 - a_odd) * (2 * pair), c)
+        return remote(rows, rows, send1.at[c, 1], recv1.at[c, 1], flipped(2))
+
+    def cross_copy(up, c):
         return remote(
-            pair_at(2 * pair if up else 0), pair_at(0 if up else 2 * pair), send1.at[3], recv1.at[2],
+            pair_at(pair, c), pair_at(0 if up else 2 * pair, c), send1.at[c, 2], recv1.at[c, 2],
+            me + 2 if up else me - 2,
+        )
+
+    def pass_copy(up, c):
+        return remote(
+            pair_at(2 * pair if up else 0, c), pair_at(0 if up else 2 * pair, c), send1.at[c, 3], recv1.at[c, 2],
             me + 4 if up else me - 4,
         )
 
-    def third_wait():
-        rows = pair_at(a_odd * (2 * pair))
-        return remote(rows, rows, send1.at[2], recv1.at[2], flipped(4))
+    def third_wait(c):
+        rows = pair_at(a_odd * (2 * pair), c)
+        return remote(rows, rows, send1.at[c, 2], recv1.at[c, 2], flipped(4))
 
     has_third = (phase == 1) | (phase == 2) | cross_up | cross_down
 
-    def halo_copy(up):
+    def halo_copy(up, c):
+        columns = columns_of(c)
         if up:
-            return remote(kv0.at[pl.ds(tok, BLOCK)], kv0.at[pl.ds(0, BLOCK)], halo_send.at[0], halo_recv.at[0], me + 1)
+            return remote(
+                kv0.at[pl.ds(tok, BLOCK), columns], kv0.at[pl.ds(0, BLOCK), columns],
+                halo_send.at[c, 0], halo_recv.at[c, 0], me + 1,
+            )
         return remote(
-            kv0.at[pl.ds(BLOCK, BLOCK)], kv0.at[pl.ds(BLOCK + tok, BLOCK)], halo_send.at[1], halo_recv.at[1], me - 1
+            kv0.at[pl.ds(BLOCK, BLOCK), columns], kv0.at[pl.ds(BLOCK + tok, BLOCK), columns],
+            halo_send.at[c, 1], halo_recv.at[c, 1], me - 1,
         )
 
-    def halo_start(wanted):
-        pl.when((me + 1 < n) & (odd == (1 - wanted)))(lambda: halo_copy(True).start())
-        pl.when((me > 0) & (odd == wanted))(lambda: halo_copy(False).start())
+    def halo_start(wanted, c):
+        pl.when((me + 1 < n) & (odd == (1 - wanted)))(lambda: halo_copy(True, c).start())
+        pl.when((me > 0) & (odd == wanted))(lambda: halo_copy(False, c).start())
 
     if spread:
-        def region(step, whose):
+        def region(step, whose, c):
             bit = bits[step]
             flips = lax.rem(lax.div(me, bit), 2)
             at = me if whose == 0 else me + bit - 2 * bit * flips
-            k, l = lax.div(at, POOL), lax.rem(at, POOL)
+            k, l = lax.div(at, POOL), inner(at)
             if bit >= POOL:
                 size = bit // POOL
-                return kv2.at[pl.ds(lax.div(k, size) * size, size), pl.ds(l, 1)]
-            return kv2.at[:, pl.ds(lax.div(l, bit) * bit, bit)]
-
-        def step_copy(step):
-            rows = region(step, 0)
-            return remote(rows, rows, send2.at[step], recv2.at[step], flipped(bits[step]))
-
-        def step_wait(step):
-            rows = region(step, 1)
-            return remote(rows, rows, send2.at[step], recv2.at[step], flipped(bits[step]))
+                return kv2.at[pl.ds(lax.div(k, size) * size, size), pl.ds(l, 1), :, columns_of(c)]
+            size = {2: 1, 1: 2, 4: 4}[bit]
+            return kv2.at[:, pl.ds(lax.div(l, size) * size, size), :, columns_of(c)]
+
+        def step_copy(step, c):
+            rows = region(step, 0, c)
+            return remote(rows, rows, send2.at[c, step], recv2.at[c, step], flipped(bits[step]))
+
+        def step_wait(step, c):
+            rows = region(step, 1, c)
+            return remote(rows, rows, send2.at[c, step], recv2.at[c, step], flipped(bits[step]))
     else:
         def over_window(act):
             @pl.loop(0, held2)
@@ -205,17 +234,22 @@
 
         def direct_copy(j, t):
             there = me - start2(t)
-            remote(slot_at(slot), slot_at(there), send2.at[j], recv2.at[there], t).start()
+            remote(slot_at(slot), slot_at(there), send2.at[0, j], recv2.at[0, there], t).start()
 
         def direct_wait(j, t):
-            return remote(slot_at(j), slot_at(j), send2.at[j], recv2.at[j], t)
-
-    half_copy().start()
-    if spread:
-        step_copy(0).start()
+            return remote(slot_at(j), slot_at(j), send2.at[0, j], recv2.at[0, j], t)
+
+    for c in range(CHUNKS):
+        half_copy(c).start()
+        if spread:
+            step_copy(0, c).start()
 
     def blank_of(own):
-        return jnp.concatenate([own[:, :WIDTH], jnp.zeros_like(own[:, WIDTH:])], axis=1)
+        parts = []
+        for h in range(KVHEADS):
+            keys = own[:, h * PER_HEAD : h * PER_HEAD + HD]
+            parts += [keys, jnp.zeros_like(keys)]
+        return jnp.concatenate(parts, axis=1)
 
     blank1 = jnp.concatenate([blank_of(pooled1)] * 2, axis=0)
 
@@ -246,7 +280,7 @@
     def _():
         kv0[pl.ds(BLOCK + tok, BLOCK), :] = blank_of(kv0[pl.ds(tok, BLOCK), :])
 
-    loads[2].wait()
+    q_load.wait()
     scale = HD ** (-0.5) * math.log2(math.e)
 
     def query(h, b):
@@ -285,7 +319,7 @@
             o_ref[pl.ds(b * BLOCK, BLOCK), pl.ds(column, HD)] = out[g * BLOCK : (g + 1) * BLOCK]
 
     def head_columns(h):
-        return pl.multiple_of(h * HD, HD), pl.multiple_of(WIDTH + h * HD, HD)
+        return pl.multiple_of(h * PER_HEAD, HD), pl.multiple_of(h * PER_HEAD + HD, HD)
 
     def fine(h, start, size, present):
         key_column, value_column = head_columns(h)
@@ -303,57 +337,63 @@
             low, high = max(b, 1), min(b + 2, blocks)
             scored(h, b, *fine(h, low * BLOCK, (high - low + 1) * BLOCK, None), True, False)
 
-    def own_loop(low, high):
-        @pl.loop(low, high)
-        def _(h):
-            own_rows(h)
-
-    if spread:
-        zs = len(bits) - 3
-        at = 0
-        for z in range(zs):
-            stop = at + 1 if at < KVHEADS else at
-            own_loop(at, stop)
-            at = stop
-            step_wait(z).wait_recv()
-            step_copy(z + 1).start()
-        half_wait().wait_recv()
-        swap_copy().start()
-        pl.when(cross_up)(lambda: cross_copy(True).start())
-        pl.when(cross_down)(lambda: cross_copy(False).start())
-        halo_start(1)
-        stop = max(at, KVHEADS - 1)
-        own_loop(at, stop)
-        step_wait(zs).wait_recv()
-        step_copy(zs + 1).start()
-        halo_start(0)
-        own_loop(stop, KVHEADS)
-    else:
+    def swap_start(c):
+        half_wait(c).wait_recv()
+        swap_copy(c).start()
+        pl.when(cross_up)(lambda: cross_copy(True, c).start())
+        pl.when(cross_down)(lambda: cross_copy(False, c).start())
+
+    def pass_start(c):
+        swap_wait(c).wait_recv()
+        pl.when(phase == 0)(lambda: pass_copy(True, c).start())
+        pl.when(phase == 3)(lambda: pass_copy(False, c).start())
+
+    def advance(step, c):
+        step_wait(step, c).wait_recv()
+        step_copy(step + 1, c).start()
+
+    chunks = range(CHUNKS)
+    last_step = len(bits) - 1 if spread else 0
+
+    if not spread:
         over_window(direct_copy)
-        half_wait().wait_recv()
-        swap_copy().start()
-        pl.when(cross_up)(lambda: cross_copy(True).start())
-        pl.when(cross_down)(lambda: cross_copy(False).start())
-        halo_start(1)
-        halo_start(0)
-        own_loop(0, KVHEADS)
-
-    swap_wait().wait_recv()
-    pl.when(phase == 0)(lambda: pass_copy(True).start())
-    pl.when(phase == 3)(lambda: pass_copy(False).start())
-    if spread:
-        step_wait(zs + 1).wait_recv()
-        step_copy(zs + 2).start()
-        step_wait(zs + 2).wait_recv()
-    else:
-        over_window(lambda j, t: direct_wait(j, t).wait_recv())
-    second = kv2[...].astype(F32).reshape(level2, 2 * WIDTH).astype(BF16)
-    kvc[pl.ds(level1, level2), :] = second
-    if spread:
-        kvc[pl.ds(top_at, top_rows), :] = pool_rows(second)
-    else:
-        loads[3].wait()
-    pl.when(has_third)(lambda: third_wait().wait_recv())
+
+    for h in range(KVHEADS):
+        if spread and 0 < h <= last_step - 2:
+            for c in chunks:
+                advance(h - 1, c)
+        if h == 2:
+            for c in chunks:
+                swap_start(c)
+        if h == KVHEADS - 1:
+            if spread:
+                for step in range(KVHEADS - 2, last_step - 1):
+                    for c in chunks:
+                        advance(step, c)
+            halo_start(1, 0)
+        own_rows(h)
+
+    def arrived(c):
+        pass_start(c)
+        halo_start(0, c)
+        if c + 1 < CHUNKS:
+            halo_start(1, c + 1)
+        if spread:
+            advance(last_step - 1, c)
+
+    def finish(c):
+        columns = columns_of(c)
+        if spread:
+            step_wait(last_step, c).wait_recv()
+        elif c == 0:
+            over_window(lambda j, t: direct_wait(j, t).wait_recv())
+        second = kv2[:, :, :, columns].astype(F32).reshape(level2, CHUNK).astype(BF16)
+        kvc[pl.ds(level1, level2), columns] = second
+        if spread:
+            kvc[pl.ds(top_at, top_rows), columns] = pool_rows(second)
+        elif c == 0:
+            loads[-1].wait()
+        pl.when(has_third)(lambda: third_wait(c).wait_recv())
 
     coarse_rows = level1 + level2 + top_rows
     row = lax.broadcasted_iota(jnp.int32, (coarse_rows, HD), 0)
@@ -367,33 +407,51 @@
         )
     coarse_count = jnp.where(missing, 0.0, 1.0).astype(BF16)
 
-    @pl.loop(0, KVHEADS)
-    def _(h):
+    def coarse(h):
         key_column, value_column = head_columns(h)
         k = kvc[:, pl.ds(key_column, HD)]
         v = jnp.concatenate([kvc[:, pl.ds(value_column, HD)], coarse_count], axis=1)
         for b in range(blocks):
             scored(h, b, k, v, False, 0 < b < blocks - 1)
 
-    pl.when(me > 0)(lambda: halo_copy(True).wait_recv())
-    pl.when(me + 1 < n)(lambda: halo_copy(False).wait_recv())
-
-    @pl.loop(0, KVHEADS)
-    def _(h):
+    def ends(h):
         scored(h, 0, *fine(h, 0, BLOCK, me > 0), False, blocks > 1)
         scored(h, blocks - 1, *fine(h, BLOCK + tok, BLOCK, me < n - 1), False, True)
 
-    pl.when(me + 1 < n)(lambda: halo_copy(True).wait_send())
-    pl.when(me > 0)(lambda: halo_copy(False).wait_send())
-    half_copy().wait_send()
-    swap_copy().wait_send()
-    pl.when(cross_up)(lambda: cross_copy(True).wait_send())
-    pl.when(cross_down)(lambda: cross_copy(False).wait_send())
-    pl.when(phase == 0)(lambda: pass_copy(True).wait_send())
-    pl.when(phase == 3)(lambda: pass_copy(False).wait_send())
+    heads = KVHEADS // CHUNKS
+    arrived(0)
+    for c in chunks:
+        finish(c)
+
+        @pl.loop(c * heads, (c + 1) * heads - 1)
+        def _(h):
+            coarse(h)
+
+        if c + 1 < CHUNKS:
+            arrived(c + 1)
+        coarse((c + 1) * heads - 1)
+
+    for c in chunks:
+        pl.when(me > 0)(lambda: halo_copy(True, c).wait_recv())
+        pl.when(me + 1 < n)(lambda: halo_copy(False, c).wait_recv())
+
+        @pl.loop(c * heads, (c + 1) * heads)
+        def _(h):
+            ends(h)
+
+    for c in chunks:
+        pl.when(me + 1 < n)(lambda: halo_copy(True, c).wait_send())
+        pl.when(me > 0)(lambda: halo_copy(False, c).wait_send())
+        half_copy(c).wait_send()
+        swap_copy(c).wait_send()
+        pl.when(cross_up)(lambda: cross_copy(True, c).wait_send())
+        pl.when(cross_down)(lambda: cross_copy(False, c).wait_send())
+        pl.when(phase == 0)(lambda: pass_copy(True, c).wait_send())
+        pl.when(phase == 3)(lambda: pass_copy(False, c).wait_send())
     if spread:
         for step in range(len(bits)):
-            step_copy(step).wait_send()
+            for c in chunks:
+                step_copy(step, c).wait_send()
     else:
         over_window(lambda j, t: direct_wait(j, t).wait_send())
 
@@ -412,7 +470,8 @@
     spread = held2 == n and n & (n - 1) == 0
     operands = [queries, keys, values]
     if not spread:
-        joined = jnp.concatenate([keys, values], axis=1)
+        heads = [x.reshape(tok, KVHEADS, HD) for x in (keys, values)]
+        joined = jnp.stack(heads, axis=2).reshape(tok, 2 * WIDTH)
         own = pool_level(pool_level(pool_level(joined)))
         operands.append(lax.all_gather(own, ("outer", "seq"), axis=0, tiled=True))
     coarse_rows = 3 * BLOCK + held2 * rows2 + n * tok // POOL**3
@@ -429,16 +488,16 @@
             pltpu.VMEM((held2 // POOL, POOL, rows2, 2 * WIDTH), BF16),
             pltpu.VMEM((units, GROUP * BLOCK, HD), F32),
             pltpu.VMEM((units, GROUP * BLOCK, 2 * HD), F32),
-            pltpu.SemaphoreType.DMA((4,)),
-            pltpu.SemaphoreType.DMA((2,)),
-            pltpu.SemaphoreType.DMA((2,)),
-            pltpu.SemaphoreType.DMA((4,)),
-            pltpu.SemaphoreType.DMA((3,)),
-            pltpu.SemaphoreType.DMA((held2,)),
-            pltpu.SemaphoreType.DMA((held2,)),
+            pltpu.SemaphoreType.DMA((2 * KVHEADS + 2,)),
+            pltpu.SemaphoreType.DMA((CHUNKS, 2)),
+            pltpu.SemaphoreType.DMA((CHUNKS, 2)),
+            pltpu.SemaphoreType.DMA((CHUNKS, 4)),
+            pltpu.SemaphoreType.DMA((CHUNKS, 3)),
+            pltpu.SemaphoreType.DMA((CHUNKS, held2)),
+            pltpu.SemaphoreType.DMA((CHUNKS, held2)),
         ],
         compiler_params=pltpu.CompilerParams(
-            collective_id=0, has_side_effects=True, vmem_limit_bytes=44 * 1024 * 1024
+            collective_id=0, has_side_effects=True, vmem_limit_bytes=58 * 1024 * 1024
         ),
     )(*operands)
 

time: 49.5 us -> 40.9 us (0.83)
  Pallas kernels: 44.3 us -> 37.2 us
  local copies, waits for them, and re-layouts: 4.99 us -> 3.16 us
    pallas_call x1, Pallas kernels: 44.3 us -> 37.2 us  [local(): pl.pallas_call(functools.partial(fused, n_seq, n_outer, spread), out_shap...]
    unnamed x7 -> x1, local copies, waits for them, and re-layouts: 4.99 us -> 3.16 us
where the time goes in v3:
time: 40.9 us; the launch traced here: 40.3 us
  Pallas kernels  37.2 us (91%)
  local copies, waits for them, and re-layouts  3.16 us (8%)
    pallas_call x1, Pallas kernels, local(): pl.pallas_call(functools.partial(fused, n_seq, n_outer, spread), out_shap...  37.2 us
    unnamed x1, local copies, waits for them, and re-layouts  3.16 us

profile of v3, /device:TPU:5, one launch (start us, length us, event | category | flops | bytes accessed | tf_op | source)
XLA Modules:
  0.0 40.3 jit_solution(8703433581493450023)
XLA Ops:
  0.0 37.2 %shard_map.37 = bf16[512,2048]{1,0:T(8,128)(2,1)} custom-call(bf16[512,2048]{1,0:T(8,128)(2,1)} %refs_0_.1, bf16[512,512]{1,0:T(8,128)(2,1)} %refs_1_.1, bf16[512,512]{1,0:T(8,128)(2,1)} %refs_2_.1), custom_call_target="tpu_custom_call" | custom-call | tf_op jit(solution)/shard_map/pallas_call | solution.py:479
  37.2 3.2 %copy.5 = bf16[512,2048]{1,0:T(8,128)(2,1)} copy(bf16[512,2048]{1,0:T(8,128)(2,1)} %shard_map.37) | data formatting | bytes 4194304
